TPU v7x, 32 devices: a whole 2x2x4 slice. The times are simulated.
32 devices in a mesh: dp: 8 (over z, y), fsdp: 4 (over x, core).
Axes of the slice: x: 2, y: 2, z: 4, core: 2. Of those that a mesh axis runs over, the one named last changes fastest.
Arguments:
- tokens: bfloat16 [3, 4, 2048, 768], P(None, 'fsdp', 'dp'), may hold values from -6 to 6
- seq_lengths: int32 [3, 4, 2], P(None, 'fsdp'), may hold values from 1 to 1920, as said below
- norm_gain: bfloat16 [768], P('fsdp'), may hold values from 0.25 to 1.75
- w_inner: bfloat16 [768, 3072], P('fsdp'), may hold values from -0.21875 to 0.21875
- w_state: bfloat16 [768, 128], P('fsdp'), may hold values from -0.078125 to 0.078125
- w_step: bfloat16 [768, 48], P('fsdp'), may hold values from -0.21875 to 0.21875
- conv_weight: bfloat16 [4, 1664], P(None, 'fsdp'), may hold values from -3 to 3
- conv_bias: bfloat16 [1664], P('fsdp'), may hold values from -3 to 3
- step_bias: bfloat16 [48], P('fsdp'), may hold values from -2 to 1
- decay_log: bfloat16 [24], P('fsdp'), may hold values from -9.1875 to -2.296875
- skip_gain: bfloat16 [24], P('fsdp'), may hold values from 0.5 to 2
- out_gain: bfloat16 [1536], P('fsdp'), may hold values from 0.25 to 1.75
- w_out: bfloat16 [1536, 768], P('fsdp'), may hold values from -0.15625 to 0.15625
- cotangent: bfloat16 [3, 4, 2048, 768], P(None, 'fsdp', 'dp'), may hold values from -6 to 6
Outputs:
- layer_out: bfloat16 [3, 4, 2048, 768], P(None, 'fsdp', 'dp')
- tokens_grad: float32 [3, 4, 2048, 768], P(None, 'fsdp', 'dp')
- norm_gain_grad: float32 [768], P('fsdp')
- w_inner_grad: float32 [768, 3072], P('fsdp')
- w_state_grad: float32 [768, 128], P('fsdp')
- w_step_grad: float32 [768, 48], P('fsdp')
- conv_weight_grad: float32 [4, 1664], P(None, 'fsdp')
- conv_bias_grad: float32 [1664], P('fsdp')
- step_bias_grad: float32 [48], P('fsdp')
- decay_log_grad: float32 [24], P('fsdp')
- skip_gain_grad: float32 [24], P('fsdp')
- out_gain_grad: float32 [1536], P('fsdp')
- w_out_grad: float32 [1536, 768], P('fsdp')
Inputs may be any that keep to these rules, and one draw needn't show every extreme that they name: Each row of seq_lengths describes one span of 2048 positions: the first sequence begins at 0, the second at the first multiple of 128 at or after the first one's end, and it ends at or before 2048. For each group, in the span of one of the 3 micro-batches, one of the two sequences begins among the first 256 positions and ends among the last 256; in every other span both sequences have 2048 // 4 tokens or more. Some sequence has exactly 1920 tokens.
All inputs are finite; a program needn't handle non-finite values.
Results may differ from a plain program's by a relative error of at most 0.0045.
The roundings to bfloat16 on the way count: a program that leaves them out, or rounds other values in their place, can miss the bound.
Values may be sent and summed in bfloat16 or wider, within the bound.
A program may use at most 576 MiB of HBM per device.

v0:
```python
from functools import partial

import jax
import jax.numpy as jnp
from jax import lax
from jax.sharding import PartitionSpec as P

INNER = 1536
HEADS = 24
HEAD_DIM = 64
STATE = 64
CONV = 4
BLOCK = 128
MB = 3
TOK_DEV = 256


EPSILON = 1e-05
HIGHEST = lax.Precision.HIGHEST


def from_behind(block, axis, distance):
    devices = range(lax.axis_size(axis))
    route = [(i - distance, i) for i in devices if i - distance in devices]
    return lax.ppermute(block, axis, route)


def carried_in(value, axis, combine, identity, reverse):
    count, index = (lax.axis_size(axis), lax.axis_index(axis))
    everything = jax.tree.map(lambda part: lax.all_gather(part, axis), value)
    start = jax.tree.map(
        lambda part, zero: jnp.broadcast_to(jnp.asarray(zero, part.dtype), part.shape),
        value,
        identity,
    )

    def lap(k, before):
        at = count - 1 - k if reverse else k
        reached = at > index if reverse else at < index
        new = combine(before, jax.tree.map(lambda part: part[at], everything))
        return jax.tree.map(lambda a, b: jnp.where(reached, a, b), new, before)

    return lax.fori_loop(0, count, lap, start)


def rms_scale(values, norm_gain):
    return (
        values * lax.rsqrt(jnp.mean(values * values, axis=-1, keepdims=True) + EPSILON) * norm_gain
    )


def span_layout(lengths, places, block_first, span_len):
    first_len = lengths[0]
    second_start = (first_len + BLOCK - 1) // BLOCK * BLOCK
    second_end = second_start + lengths[1]
    inside = (places < first_len) | (places >= second_start) & (places < second_end)
    valid_mask = inside.astype(jnp.float32)
    offset = jnp.where(places >= second_start, places - second_start, places)

    def begins(position):
        return ((position == 0) | (position == second_start) | (position >= span_len)).astype(
            jnp.float32
        )

    return (valid_mask, offset, 1.0 - begins(block_first), 1.0 - begins(block_first + BLOCK))


def mixer_inputs(
    conv_in, before, dt_raw, conv_weight, conv_bias, step_bias, decay_log, valid_mask, offset
):
    rows_count = conv_in.shape[0]
    padded = jnp.concatenate([before, conv_in], axis=0)
    conv_out = conv_bias + jnp.zeros_like(conv_in)
    for lag_index in range(CONV):
        window = padded[CONV - 1 - lag_index : CONV - 1 - lag_index + rows_count]
        conv_out = (
            conv_out
            + conv_weight[lag_index] * window * (offset >= lag_index).astype(jnp.float32)[:, None]
        )
    activated = valid_mask[:, None] * jax.nn.silu(conv_out)
    head_vals = activated[:, :INNER].reshape(rows_count, HEADS, HEAD_DIM)
    state_in = activated[:, INNER : INNER + STATE]
    state_out = activated[:, INNER + STATE :]
    step_sizes = jax.nn.softplus(dt_raw + step_bias)
    decay_rates = jnp.exp(decay_log)
    fwd_step = step_sizes[:, :HEADS]
    rev_step = step_sizes[:, HEADS:]
    return (
        head_vals,
        state_in,
        state_out,
        fwd_step,
        rev_step,
        -fwd_step * decay_rates,
        -rev_step * decay_rates,
    )


def block_sums(fwd_log, rev_log):
    fwd_cum = jnp.cumsum(fwd_log, axis=0)
    rev_cum = jnp.flip(jnp.cumsum(jnp.flip(rev_log, 0), axis=0), 0)
    return (fwd_cum, rev_cum)


def block_states(head_vals, state_in, fwd_step, rev_step, fwd_log, rev_log):
    fwd_cum, rev_cum = block_sums(fwd_log, rev_log)
    fwd_tail = jnp.exp(fwd_cum[-1:] - fwd_cum) * fwd_step
    rev_head = jnp.exp(rev_cum[:1] - rev_cum) * rev_step
    fwd_state = jnp.einsum("sh,sn,shp->hnp", fwd_tail, state_in, head_vals, precision=HIGHEST)
    rev_state = jnp.einsum("sh,sn,shp->hnp", rev_head, state_in, head_vals, precision=HIGHEST)
    return (fwd_state, jnp.exp(fwd_cum[-1]), rev_state, jnp.exp(rev_cum[0]))


def block_output(
    head_vals, state_in, state_out, fwd_step, rev_step, fwd_log, rev_log, fwd_enter, rev_enter
):
    fwd_cum, rev_cum = block_sums(fwd_log, rev_log)
    positions = jnp.arange(head_vals.shape[0], dtype=jnp.int32)
    lower_mask = (positions[:, None] > positions[None, :])[:, :, None]
    upper_mask = (positions[:, None] < positions[None, :])[:, :, None]
    fwd_gap = fwd_cum[:, None, :] - fwd_cum[None, :, :]
    rev_gap = rev_cum[:, None, :] - rev_cum[None, :, :]
    scores = jnp.dot(state_out, state_in.T, precision=HIGHEST)
    mixing = jnp.where(
        lower_mask, jnp.exp(jnp.where(lower_mask, fwd_gap, 0.0)) * fwd_step[None], 0.0
    )
    mixing = mixing + jnp.where(
        upper_mask, jnp.exp(jnp.where(upper_mask, rev_gap, 0.0)) * rev_step[None], 0.0
    )
    mixing = mixing * scores[:, :, None]
    inner_part = jnp.einsum("tsh,shp->thp", mixing, head_vals, precision=HIGHEST)
    carried = (
        jnp.einsum("tn,hnp->thp", state_out, fwd_enter, precision=HIGHEST)
        * jnp.exp(fwd_cum)[:, :, None]
    )
    carried = (
        carried
        + jnp.einsum("tn,hnp->thp", state_out, rev_enter, precision=HIGHEST)
        * jnp.exp(rev_cum)[:, :, None]
    )
    return inner_part + carried


def walk_block(running, block_item):
    state_part, decay_part, keep_part = block_item
    entering = keep_part * running
    return (decay_part[:, None, None] * entering + state_part, entering)


def fold_block(running, block_item):
    running_gain, running_state = running
    state_part, decay_part, keep_part = block_item
    factor = decay_part * keep_part
    return ((running_gain * factor, factor[:, None, None] * running_state + state_part), None)


def combine_states(earlier, later):
    later_gain = later[0]
    return (earlier[0] * later_gain, later_gain[:, None, None] * earlier[1] + later[1])


def front_pass(
    conv_in,
    before,
    dt_raw,
    conv_weight,
    conv_bias,
    step_bias,
    decay_log,
    valid_mask,
    offset,
    keep_fwd,
    keep_rev,
):
    mixer_parts = mixer_inputs(
        conv_in, before, dt_raw, conv_weight, conv_bias, step_bias, decay_log, valid_mask, offset
    )
    block_count = keep_fwd.shape[0]
    blocks = tuple(
        (member.reshape((block_count, BLOCK) + member.shape[1:]) for member in mixer_parts)
    )
    fwd_state, fwd_decay, rev_state, rev_decay = jax.vmap(block_states)(
        blocks[0], blocks[1], blocks[3], blocks[4], blocks[5], blocks[6]
    )
    initial = (jnp.ones((HEADS,), jnp.float32), jnp.zeros((HEADS, STATE, HEAD_DIM), jnp.float32))
    (fwd_gain, fwd_total), _ = lax.scan(fold_block, initial, (fwd_state, fwd_decay, keep_fwd))
    (rev_gain, rev_total), _ = lax.scan(
        fold_block, initial, (rev_state, rev_decay, keep_rev), reverse=True
    )
    return (
        blocks,
        (fwd_state, fwd_decay, rev_state, rev_decay),
        (fwd_gain, fwd_total, rev_gain, rev_total),
    )


def output_pass(
    blocks, local_sums, fwd_enter, rev_enter, gate_in, skip_gain, out_gain, keep_fwd, keep_rev
):
    fwd_state, fwd_decay, rev_state, rev_decay = local_sums
    _, fwd_in = lax.scan(walk_block, fwd_enter, (fwd_state, fwd_decay, keep_fwd))
    _, rev_in = lax.scan(walk_block, rev_enter, (rev_state, rev_decay, keep_rev), reverse=True)
    mixed = jax.vmap(block_output)(*blocks + (fwd_in, rev_in))
    rows_count = gate_in.shape[0]
    mixed = mixed.reshape(rows_count, HEADS, HEAD_DIM) + skip_gain[None, :, None] * blocks[
        0
    ].reshape(rows_count, HEADS, HEAD_DIM)
    gated = mixed.reshape(rows_count, INNER) * jax.nn.silu(gate_in)
    return rms_scale(gated, out_gain)


def contract_rows(left, right):
    return lax.dot_general(
        left, right, (((0,), (0,)), ((), ())), preferred_element_type=jnp.float32
    )


def contract_cols(left, right):
    return lax.dot_general(
        left, right, (((1,), (1,)), ((), ())), preferred_element_type=jnp.float32
    )


def on_device(
    tokens,
    seq_lengths,
    norm_gain,
    w_inner,
    w_state,
    w_step,
    conv_weight,
    conv_bias,
    step_bias,
    decay_log,
    skip_gain,
    out_gain,
    w_out,
    cotangent,
):
    shards = (
        norm_gain,
        w_inner,
        w_state,
        w_step,
        conv_weight,
        conv_bias,
        step_bias,
        decay_log,
        skip_gain,
        out_gain,
        w_out,
    )
    dp_count = lax.axis_size("dp")
    dp_rank = lax.axis_index("dp")
    span_len = TOK_DEV * dp_count
    places = dp_rank * TOK_DEV + jnp.arange(TOK_DEV, dtype=jnp.int32)
    block_first = dp_rank * TOK_DEV + jnp.arange(TOK_DEV // BLOCK, dtype=jnp.int32) * BLOCK
    tail_rows = CONV - 1
    out_list = []
    grad_list = []
    totals = None
    for micro_index in range(MB):
        full = (
            lax.all_gather(shards[0], "fsdp", axis=0, tiled=True),
            lax.all_gather(shards[1], "fsdp", axis=0, tiled=True),
            lax.all_gather(shards[2], "fsdp", axis=0, tiled=True),
            lax.all_gather(shards[3], "fsdp", axis=0, tiled=True),
            lax.all_gather(shards[4], "fsdp", axis=1, tiled=True),
            lax.all_gather(shards[5], "fsdp", axis=0, tiled=True),
            lax.all_gather(shards[6], "fsdp", axis=0, tiled=True),
            lax.all_gather(shards[7], "fsdp", axis=0, tiled=True),
            lax.all_gather(shards[8], "fsdp", axis=0, tiled=True),
            lax.all_gather(shards[9], "fsdp", axis=0, tiled=True),
            lax.all_gather(shards[10], "fsdp", axis=0, tiled=True),
        )
        small = tuple(
            (full[index_small].astype(jnp.float32) for index_small in (0, 4, 5, 6, 7, 8, 9))
        )
        gain_in, weight_conv, bias_conv, bias_steps, log_decay, gain_skip, gain_out = small
        lengths = seq_lengths[micro_index, 0]
        valid_mask, offset, keep_fwd, keep_rev = span_layout(lengths, places, block_first, span_len)
        x_rows = tokens[micro_index, 0].astype(jnp.float32)
        hidden, rms_back = jax.vjp(rms_scale, x_rows, gain_in)
        hidden_low = hidden.astype(jnp.bfloat16)
        proj_zx = jnp.dot(hidden_low, full[1], preferred_element_type=jnp.float32)
        proj_bc = jnp.dot(hidden_low, full[2], preferred_element_type=jnp.float32)
        dt_raw = jnp.dot(hidden_low, full[3], preferred_element_type=jnp.float32)
        gate_in = proj_zx[:, :INNER]
        conv_in = jnp.concatenate([proj_zx[:, INNER:], proj_bc], axis=1)
        before = from_behind(conv_in[TOK_DEV - tail_rows :], "dp", 1)
        front_fn = partial(
            front_pass, valid_mask=valid_mask, offset=offset, keep_fwd=keep_fwd, keep_rev=keep_rev
        )
        front_out, front_back = jax.vjp(
            front_fn, conv_in, before, dt_raw, weight_conv, bias_conv, bias_steps, log_decay
        )
        blocks, local_sums, device_sums = front_out
        fwd_gain, fwd_total, rev_gain, rev_total = device_sums
        identity = (jnp.ones_like(fwd_gain), jnp.zeros_like(fwd_total))
        fwd_enter = carried_in((fwd_gain, fwd_total), "dp", combine_states, identity, False)[1]
        rev_enter = carried_in((rev_gain, rev_total), "dp", combine_states, identity, True)[1]
        output_fn = partial(output_pass, keep_fwd=keep_fwd, keep_rev=keep_rev)
        normed, output_back = jax.vjp(
            output_fn, blocks, local_sums, fwd_enter, rev_enter, gate_in, gain_skip, gain_out
        )
        normed_low = normed.astype(jnp.bfloat16)
        branch = jnp.dot(normed_low, full[10], preferred_element_type=jnp.float32)
        out_list.append((valid_mask[:, None] * (x_rows + branch)).astype(jnp.bfloat16))
        back = (
            lax.all_gather(shards[0], "fsdp", axis=0, tiled=True),
            lax.all_gather(shards[1], "fsdp", axis=0, tiled=True),
            lax.all_gather(shards[2], "fsdp", axis=0, tiled=True),
            lax.all_gather(shards[3], "fsdp", axis=0, tiled=True),
            lax.all_gather(shards[4], "fsdp", axis=1, tiled=True),
            lax.all_gather(shards[5], "fsdp", axis=0, tiled=True),
            lax.all_gather(shards[6], "fsdp", axis=0, tiled=True),
            lax.all_gather(shards[7], "fsdp", axis=0, tiled=True),
            lax.all_gather(shards[8], "fsdp", axis=0, tiled=True),
            lax.all_gather(shards[9], "fsdp", axis=0, tiled=True),
            lax.all_gather(shards[10], "fsdp", axis=0, tiled=True),
        )
        cot_rows = cotangent[micro_index, 0]
        d_branch = cot_rows * valid_mask[:, None].astype(jnp.bfloat16)
        grad_w_out = contract_rows(normed_low, d_branch)
        d_normed = contract_cols(d_branch, back[10])
        d_blocks, d_local, d_fwd_enter, d_rev_enter, d_gate_in, d_skip, d_out_gain = output_back(
            d_normed
        )
        fwd_after = carried_in((fwd_gain, d_fwd_enter), "dp", combine_states, identity, True)[1]
        rev_after = carried_in((rev_gain, d_rev_enter), "dp", combine_states, identity, False)[1]
        d_device = (
            jnp.sum(fwd_after * fwd_enter, axis=(1, 2)),
            fwd_after,
            jnp.sum(rev_after * rev_enter, axis=(1, 2)),
            rev_after,
        )
        d_conv_in, d_before, d_dt_raw, d_conv_weight, d_conv_bias, d_step_bias, d_decay_log = (
            front_back((d_blocks, d_local, d_device))
        )
        from_next = from_behind(d_before, "dp", -1)
        d_conv_in = jnp.concatenate(
            [d_conv_in[: TOK_DEV - tail_rows], d_conv_in[TOK_DEV - tail_rows :] + from_next], axis=0
        )
        d_zx = jnp.concatenate([d_gate_in, d_conv_in[:, :INNER]], axis=1).astype(jnp.bfloat16)
        d_bc = d_conv_in[:, INNER:].astype(jnp.bfloat16)
        d_steps = d_dt_raw.astype(jnp.bfloat16)
        grad_w_inner = contract_rows(hidden_low, d_zx)
        grad_w_state = contract_rows(hidden_low, d_bc)
        grad_w_step = contract_rows(hidden_low, d_steps)
        d_hidden = (
            contract_cols(d_zx, back[1])
            + contract_cols(d_bc, back[2])
            + contract_cols(d_steps, back[3])
        )
        d_x_norm, d_norm_gain = rms_back(d_hidden)
        grad_list.append(d_x_norm + valid_mask[:, None] * cot_rows.astype(jnp.float32))
        grads = (
            d_norm_gain,
            grad_w_inner,
            grad_w_state,
            grad_w_step,
            d_conv_weight,
            d_conv_bias,
            d_step_bias,
            d_decay_log,
            d_skip,
            d_out_gain,
            grad_w_out,
        )
        totals = grads if micro_index == 0 else jax.tree.map(jnp.add, totals, grads)
    summed = lax.psum(totals, "dp")
    owned = (
        lax.psum_scatter(summed[0], "fsdp", scatter_dimension=0, tiled=True),
        lax.psum_scatter(summed[1], "fsdp", scatter_dimension=0, tiled=True),
        lax.psum_scatter(summed[2], "fsdp", scatter_dimension=0, tiled=True),
        lax.psum_scatter(summed[3], "fsdp", scatter_dimension=0, tiled=True),
        lax.psum_scatter(summed[4], "fsdp", scatter_dimension=1, tiled=True),
        lax.psum_scatter(summed[5], "fsdp", scatter_dimension=0, tiled=True),
        lax.psum_scatter(summed[6], "fsdp", scatter_dimension=0, tiled=True),
        lax.psum_scatter(summed[7], "fsdp", scatter_dimension=0, tiled=True),
        lax.psum_scatter(summed[8], "fsdp", scatter_dimension=0, tiled=True),
        lax.psum_scatter(summed[9], "fsdp", scatter_dimension=0, tiled=True),
        lax.psum_scatter(summed[10], "fsdp", scatter_dimension=0, tiled=True),
    )
    layer_out = jnp.stack(out_list)[:, None]
    tokens_grad = jnp.stack(grad_list)[:, None]
    return (layer_out, tokens_grad) + tuple(owned)


def solution(mesh):
    placed = (
        P(None, "fsdp", "dp", None),
        P(None, "fsdp", None),
        P("fsdp"),
        P("fsdp", None),
        P("fsdp", None),
        P("fsdp", None),
        P(None, "fsdp"),
        P("fsdp"),
        P("fsdp"),
        P("fsdp"),
        P("fsdp"),
        P("fsdp"),
        P("fsdp", None),
        P(None, "fsdp", "dp", None),
    )
    return jax.shard_map(
        on_device,
        mesh=mesh,
        in_specs=placed,
        out_specs=(
            P(None, "fsdp", "dp", None),
            P(None, "fsdp", "dp", None),
            P("fsdp"),
            P("fsdp", None),
            P("fsdp", None),
            P("fsdp", None),
            P(None, "fsdp"),
            P("fsdp"),
            P("fsdp"),
            P("fsdp"),
            P("fsdp"),
            P("fsdp"),
            P("fsdp", None),
        ),
        check_vma=False,
    )
```

profile of v0, /device:TPU:0, one launch (start us, length us, event | category | flops | bytes accessed | tf_op | source)
XLA Modules:
  0.0 1825.4 jit_solution(11417034793801359791)
XLA Ops:
  205.5 15.3 while.646
  259.5 24.4 %all-reduce.69 = (f32[192]{0:T(256)S(1)}, f32[192]{0:T(256)S(1)}, f32[192]{0:T(256)S(1)}, f32[192]{0:T(256)S(1)}, f32[192]{0:T(256)S(1)}, /*index=5*/f32[192]{0:T(256)S(1)}) all-reduce(f32[192]{0:T(256)S(1)} %dynamic-update-slice.10, f32[192]{0:T(256)S(1)} %dynamic-update-slice.9, ...), channel_id=12, replica_groups=mesh['dp'=8,'fsdp'=4] {'dp'}, use_global_device_ids=true, to_apply=%add.61 | all-reduce | flops 1152 | bytes 9216
  290.8 11.0 while.639
  354.0 30.8 %all-gather.46.cloned.1.call-done = f32[192,64,64]{2,1,0:T(8,128)} async-done(((f32[24,64,64]{2,1,0:T(8,128)}), f32[192,64,64]{2,1,0:T(8,128)}) %all-gather.46.cloned.1.call-update) | async-done | bytes 3145744 | tf_op jit(solution)/shard_map/all_gather | solution.py:30
  416.0 68.1 %all-gather.44.cloned.1.call-done = f32[192,64,64]{2,1,0:T(8,128)} async-done(((f32[24,64,64]{2,1,0:T(8,128)}), f32[192,64,64]{2,1,0:T(8,128)}) %all-gather.44.cloned.1.call-update) | async-done | bytes 3145744 | tf_op jit(solution)/shard_map/all_gather | solution.py:30
  547.0 36.5 %all-gather.50.cloned.1.call-done = f32[192,64,64]{2,1,0:T(8,128)} async-done(((f32[24,64,64]{2,1,0:T(8,128)}), f32[192,64,64]{2,1,0:T(8,128)}) %all-gather.50.cloned.1.call-update) | async-done | bytes 3145744 | tf_op jit(solution)/shard_map/all_gather | solution.py:30
  583.5 10.9 while.647
  597.1 12.3 while.629
  615.1 68.4 %all-gather.48.cloned.1.call-done = f32[192,64,64]{2,1,0:T(8,128)} async-done(((f32[24,64,64]{2,1,0:T(8,128)}), f32[192,64,64]{2,1,0:T(8,128)}) %all-gather.48.cloned.1.call-update) | async-done | bytes 3145744 | tf_op jit(solution)/shard_map/all_gather | solution.py:30
  698.7 11.8 while.628
  758.4 19.0 %while.656 = (s32[]{:T(128)}, f32[24,64,64]{2,1,0:T(8,128)}, f32[2,24,64,64]{3,2,1,0:T(8,128)}, f32[2,24]{1,0:T(2,128)S(1)}, f32[2]{0:T(128)}, /*index=5*/f32[2,...) while((s32[]{:T(128)}, f32[24,64,64]{2,1,0:T(8,128)}, ...), condition=%wide.region_122.124_spmd.clone, body=%wide.region_120.123_spmd.clone.sunk | while | flops 688107 | bytes 18088780 | solution.py:202
  789.4 13.8 while.648
  809.6 13.5 while.658
  828.2 13.7 while.650
  862.0 16.0 fusion.156
  885.3 21.4 %while.652 = (s32[]{:T(128)}, f32[24,64,64]{2,1,0:T(8,128)}, f32[2,24,64,64]{3,2,1,0:T(8,128)}, f32[2,24]{1,0:T(2,128)S(1)}, f32[2]{0:T(128)S(1)}, /*index=5*/f3...) while((s32[]{:T(128)}, f32[24,64,64]{2,1,0:T(8,128)}, ...), condition=%wide.region_87.89_spmd.clone, body=%wide.region_85.88_spmd.clone.sunk | while | flops 688107 | bytes 11797268 | solution.py:202
  915.2 12.0 fusion.152
  955.8 21.6 %while.654 = (s32[]{:T(128)}, f32[24,64,64]{2,1,0:T(8,128)}, f32[2,24,64,64]{3,2,1,0:T(8,128)}, f32[2,24]{1,0:T(2,128)S(1)}, f32[2]{0:T(128)S(1)}, /*index=5*/f3...) while((s32[]{:T(128)}, f32[24,64,64]{2,1,0:T(8,128)}, ...), condition=%wide.region_96.98_spmd.clone, body=%wide.region_94.97_spmd.clone.sunk | while | flops 688108 | bytes 11797280 | solution.py:201
  978.0 24.9 %while.657 = (s32[]{:T(128)}, f32[24,64,64]{2,1,0:T(8,128)}, s32[]{:T(128)}, f32[8,24]{1,0:T(8,128)}, f32[8,24,64,64]{3,2,1,0:T(8,128)}, /*index=5*/s32[]{:T(128)}, s32[]{:T(128)}) while((s32[]{:T(128)}, f32[24,64,64]{2,1,0:T(8,128)}, s32[]{:T(128)}, f32[8,24]{1,0:T(8,128)}, f32[8,24,64,64]{3,2,1,0:T(8,128)}, ...), condition=%wide.region_124.126_spmd.clone, body=%wide.region_123.125_spmd.clone.sunk | while | flops 393220 | bytes 1180049 | solution.py:43
  1026.0 16.0 while.649
  1073.5 24.9 %while.659 = (s32[]{:T(128)}, f32[24,64,64]{2,1,0:T(8,128)}, s32[]{:T(128)}, f32[8,24]{1,0:T(8,128)}, f32[8,24,64,64]{3,2,1,0:T(8,128)}, /*index=5*/s32[]{:T(128)}, s32[]{:T(128)}, s32[]{:T(128)}, s32[]{:T(128)}) while((s32[]{:T(128)}, f32[24,64,64]{2,1,0:T(8,128)}, s32[]{:T(128)}, f32[8,24]{1,0:T(8,128)}, ...), condition=%wide.region_133.135_spmd.clone, body=%wide.region_132.134_spmd.clone.sunk | while | flops 393224 | bytes 1180111 | solution.py:43
  1101.2 12.4 while.635
  1132.7 40.1 %all-gather.54.cloned.1.call-done = f32[192,64,64]{2,1,0:T(8,128)} async-done(((f32[24,64,64]{2,1,0:T(8,128)}), f32[192,64,64]{2,1,0:T(8,128)}) %all-gather.54.cloned.1.call-update) | async-done | bytes 3145744 | tf_op jit(solution)/shard_map/all_gather | solution.py:30
  1172.8 24.7 %while.651 = (s32[]{:T(128)}, f32[24,64,64]{2,1,0:T(8,128)}, s32[]{:T(128)}, f32[8,24]{1,0:T(8,128)}, f32[8,24,64,64]{3,2,1,0:T(8,128)}, /*index=5*/s32[]{:T(128)}, s32[]{:T(128)}, s32[]{:T(128)}, s32[]{:T(128)}) while((s32[]{:T(128)}, f32[24,64,64]{2,1,0:T(8,128)}, s32[]{:T(128)}, f32[8,24]{1,0:T(8,128)}, ...), condition=%wide.region_63.65_spmd.clone, body=%wide.region_62.64_spmd.clone.sunk | while | flops 393224 | bytes 1180111 | solution.py:43
  1200.3 12.6 while.631
  1231.6 40.7 %all-gather.56.cloned.1.call-done = f32[192,64,64]{2,1,0:T(8,128)} async-done(((f32[24,64,64]{2,1,0:T(8,128)}), f32[192,64,64]{2,1,0:T(8,128)}) %all-gather.56.cloned.1.call-update) | async-done | bytes 3145744 | tf_op jit(solution)/shard_map/all_gather | solution.py:30
  1272.2 16.2 while.653
  1308.0 63.5 %all-gather.58.cloned.1.call-done = f32[192,64,64]{2,1,0:T(8,128)} async-done(((f32[24,64,64]{2,1,0:T(8,128)}), f32[192,64,64]{2,1,0:T(8,128)}) %all-gather.58.cloned.1.call-update) | async-done | bytes 3145744 | tf_op jit(solution)/shard_map/all_gather | solution.py:30
  1371.5 16.4 while.655
  1654.9 11.1 reduce-scatter.16.cloned.1.call-done
  1667.0 40.4 %all-reduce.68 = (f32[192]{0:T(256)}, f32[192,48]{0,1:T(8,128)}, f32[4,416]{1,0:T(4,128)}, f32[416]{0:T(512)}, f32[12]{0:T(128)}, /*index=5*/f32[6]{0:T(128)}, f32[6]{0:T(128)}, f32[384]{0:T(512)}) all-reduce(f32[192]{0:T(256)S(1)} %dynamic-slice.12, f32[192,48]{0,1:T(8,128)S(1)} %copy.1319, ...), channel_id=1, replica_groups=mesh['dp'=8,'fsdp'=4] {'dp'}, use_global_device_ids=true, to_apply=%region_156.158 | all-reduce | flops 11896 | bytes 95168 | tf_op jit(solution)/shard_map/psum | solution.py:371
  1707.4 105.8 %all-reduce.75.cloned.1.call-done = (f32[192,3072]{1,0:T(8,128)}, f32[192,128]{1,0:T(8,128)}, f32[384,768]{1,0:T(8,128)}) async-done(((f32[192,3072]{1,0:T(8,128)}, f32[192,128]{1,0:T(8,128)}, f32[384,768]{1,0:T(8,128)}), (f32[192,3072]{1,0:T(8,128)}, f32[192,128]{1,0:T(8,128)}, f32[384,768]{1,0:T(8,128)})) %all-reduce.75.cloned.1.call-update) | async-done | bytes 3637264 | tf_op jit(solution)/shard_map/psum | solution.py:371
  (2536 shorter events, 1383.7 us)
Async XLA Ops:
  7.3 44.3 %all-gather.36.cloned.1.call-start = ((), (), s32[]{:S(2)}) async-start(), calls=%async_computation.5 | async-start | bytes 5898240 | tf_op jit(solution)/shard_map/all_gather | solution.py:265
  8.0 229.2 %all-gather.38.cloned.1.call-start = ((), (), s32[]{:S(2)}) async-start(), calls=%async_computation.6 | async-start | bytes 2949120 | tf_op jit(solution)/shard_map/all_gather | solution.py:274
  8.8 282.0 %all-gather.42.cloned.1.call-start = ((), (), s32[]{:S(2)}) async-start(), calls=%async_computation.8 | async-start | bytes 7077888 | tf_op jit(solution)/shard_map/all_gather | solution.py:30
  23.7 144.2 %copy-start.232 = (f32[768]{0:T(1024)}, f32[768]{0:T(1024)S(1)}, u32[]{:S(2)}) copy-start(f32[768]{0:T(1024)S(1)} %convert_element_type.265) | copy-start | bytes 9220
  30.7 74.2 %copy-start.381 = (f32[256]{0:T(256)}, f32[256]{0:T(256)S(1)}, u32[]{:S(2)}) copy-start(f32[256]{0:T(256)S(1)} %get-tuple-element.6006) | copy-start | bytes 3076
  57.1 4.9 collective-permute-start
  71.4 440.5 %copy-start.19 = (f32[2,128,24,64]{1,3,2,0:T(8,128)}, f32[2,128,24,64]{1,3,2,0:T(8,128)S(1)}, u32[]{:S(2)}) copy-start(f32[2,128,24,64]{1,3,2,0:T(8,128)S(1)} %copy.1003) | copy-start | bytes 4718596
  84.8 237.9 %all-gather.40.cloned.1.call-start = ((), (), s32[]{:S(2)}) async-start(), calls=%async_computation.7 | async-start | bytes 7077888 | tf_op jit(solution)/shard_map/all_gather | solution.py:30
  98.1 286.7 %all-gather.46.cloned.1.call-start = ((), (), s32[]{:S(2)}) async-start(), calls=%async_computation.10 | async-start | bytes 7077888 | tf_op jit(solution)/shard_map/all_gather | solution.py:30
  111.7 5.7 collective-permute-start.1
  146.8 337.3 %all-gather.44.cloned.1.call-start = ((), (), s32[]{:S(2)}) async-start(), calls=%async_computation.9 | async-start | bytes 7077888 | tf_op jit(solution)/shard_map/all_gather | solution.py:30
  161.7 421.8 %all-gather.50.cloned.1.call-start = ((), (), s32[]{:S(2)}) async-start(), calls=%async_computation.12 | async-start | bytes 7077888 | tf_op jit(solution)/shard_map/all_gather | solution.py:30
  174.8 5.8 collective-permute-start.2
  221.8 461.7 %all-gather.48.cloned.1.call-start = ((), (), s32[]{:S(2)}) async-start(), calls=%async_computation.11 | async-start | bytes 7077888 | tf_op jit(solution)/shard_map/all_gather | solution.py:30
  235.4 697.1 %copy-start.292 = (f32[1536]{0:T(1024)}, f32[1536]{0:T(1024)S(1)}, u32[]{:S(2)}) copy-start(f32[1536]{0:T(1024)S(1)} %reshape.1006) | copy-start | bytes 18436
  290.3 687.2 %all-gather.60.cloned.1.call-start = ((), (), s32[]{:S(2)}) async-start(), calls=%async_computation.17 | async-start | bytes 7077888 | tf_op jit(solution)/shard_map/all_gather | solution.py:30
  611.1 72.5 %copy-start.64 = (f32[24,64,64]{2,1,0:T(8,128)S(1)}, f32[24,64,64]{2,1,0:T(8,128)}, u32[]{:S(2)}) copy-start(f32[24,64,64]{2,1,0:T(8,128)} %custom-call.14) | copy-start | bytes 1179652
  737.3 195.2 %copy-start.504 = (f32[256]{0:T(256)}, f32[256]{0:T(256)S(1)}, u32[]{:S(2)}) copy-start(f32[256]{0:T(256)S(1)} %fusion.474) | copy-start | bytes 3076
  777.4 248.6 %all-gather.52.cloned.1.call-start = ((), (), s32[]{:S(2)}) async-start(), calls=%async_computation.13 | async-start | bytes 7077888 | tf_op jit(solution)/shard_map/all_gather | solution.py:30
  804.1 269.4 %all-gather.62.cloned.1.call-start = ((), (), s32[]{:S(2)}) async-start(), calls=%async_computation.18 | async-start | bytes 7077888 | tf_op jit(solution)/shard_map/all_gather | solution.py:30
  824.1 348.7 %all-gather.54.cloned.1.call-start = ((), (), s32[]{:S(2)}) async-start(), calls=%async_computation.14 | async-start | bytes 7077888 | tf_op jit(solution)/shard_map/all_gather | solution.py:30
  842.9 429.4 %all-gather.56.cloned.1.call-start = ((), (), s32[]{:S(2)}) async-start(), calls=%async_computation.15 | async-start | bytes 7077888 | tf_op jit(solution)/shard_map/all_gather | solution.py:30
  906.7 464.8 %all-gather.58.cloned.1.call-start = ((), (), s32[]{:S(2)}) async-start(), calls=%async_computation.16 | async-start | bytes 7077888 | tf_op jit(solution)/shard_map/all_gather | solution.py:30
  977.4 646.5 %reduce-scatter.12.cloned.1.call-start = ((), (), s32[]{:S(2)}) async-start(), calls=%async_computation.20 | async-start | bytes 491520 | tf_op jit(solution)/shard_map/reduce_scatter | solution.py:375
  1434.3 5.7 collective-permute-start.4
  1436.2 6.4 collective-permute-start.3
  1437.9 7.0 collective-permute-start.5
  1446.8 177.1 %reduce-scatter.14.cloned.1.call-start = ((), (), s32[]{:S(2)}) async-start(), calls=%async_computation.21 | async-start | bytes 5898240 | tf_op jit(solution)/shard_map/reduce_scatter | solution.py:383
  1455.1 168.8 %reduce-scatter.10.cloned.1.call-start = ((), (), s32[]{:S(2)}) async-start(), calls=%async_computation.19 | async-start | bytes 11796480 | tf_op jit(solution)/shard_map/reduce_scatter | solution.py:374
  1468.2 185.7 %reduce-scatter.18.cloned.1.call-start = ((), (), s32[]{:S(2)}) async-start(), calls=%async_computation.23 | async-start | bytes 1064960
  1617.4 48.6 %reduce-scatter.16.cloned.1.call-start = ((), (), s32[]{:S(2)}) async-start(), calls=%async_computation.22 | async-start | bytes 491520
  1619.6 193.7 %all-reduce.75.cloned.1.call-start = ((), (), s32[]{:S(2)}) async-start(), calls=%async_computation.24 | async-start | bytes 7274496 | tf_op jit(solution)/shard_map/psum | solution.py:371
  (676 other events, 4197.6 us)
Sparse Core Ops, SparseCore 0:
  9.7 41.8 all-gather.35
  53.2 24.0 all-gather.37
  84.9 100.4 all-gather.41
  187.4 97.8 all-gather.39
  287.4 97.3 all-gather.45
  386.8 97.2 all-gather.43
  486.3 97.1 all-gather.49
  586.3 97.1 all-gather.47
  777.6 97.2 all-gather.59
  876.8 97.1 all-gather.51
  976.3 97.2 all-gather.61
  1075.6 97.1 all-gather.53
  1175.0 97.1 all-gather.55
  1274.3 97.1 all-gather.57
  1446.9 22.4 reduce-scatter.11
  1471.8 47.8 reduce-scatter.13
  1522.3 78.3 reduce-scatter.9
  1617.5 25.1 reduce-scatter.17
  1645.2 20.8 reduce-scatter.15
  1669.8 143.4 all-reduce.74
where the time goes:
time: 1850 us; the launch traced here: 1830 us
  waiting for transfers between devices  487 us (26%)
  local copies, waits for them, and re-layouts  439 us (24%)
  other arithmetic  411 us (22%)
  matrix products  325 us (18%)
  blocking collectives  107 us (6%)
  between operations  32.3 us (2%)
    all_gather x12, waiting for transfers between devices, carried_in(): everything = jax.tree.map(lambda part: lax.all_gather(part, axis), value)  359 us
    select_n x96, other arithmetic, lap(): return jax.tree.map(lambda a, b: jnp.where(reached, a, b), new, before)  152 us
    psum x1, waiting for transfers between devices, on_device(): summed = lax.psum(totals, 'dp')  106 us
    dot_general x9, matrix products, block_output(): jnp.einsum('tsh,shp->thp', mixing, head_vals, precision=HIGHEST)  77.4 us
    dynamic_slice x72, local copies, waits for them, and re-layouts, front_pass(): lax.scan(fold_block, initial, (fwd_state, fwd_decay, keep_fwd))  68.2 us
    dot_general x12, matrix products, block_states(): jnp.einsum('sh,sn,shp->hnp', fwd_tail, state_in, head_vals, precision=HIG...  66.8 us
    unnamed x1213, local copies, waits for them, and re-layouts  58.5 us
    while x220, local copies, waits for them, and re-layouts  58.5 us
  transfers between devices with their start and end apart: 26, of which 17 were waited for; matrix products, arithmetic and copies ran while one was open for 52% of the time, Pallas kernels for 0%

commit v1 on v0

v1 whole, which is shorter than its diff:
```python
from functools import partial

import jax
import jax.numpy as jnp
from jax import lax
from jax.experimental import pallas as pl
from jax.experimental.pallas import tpu as pltpu
from jax.sharding import PartitionSpec as P

D = 768
INNER = 1536
HEADS = 24
HEAD_DIM = 64
STATE = 64
CONV = 4
BLOCK = 128
MB = 3
TOK_DEV = 256
HALO = 8
LANES = 128
CONV_COLS = INNER + 2 * STATE
WIDE = 2 * INNER + 2 * LANES
LATE = INNER + 2 * LANES
PAIRS = HEADS // 2
PARTS = 2
CHUNKS = MB * PARTS
EPSILON = 1e-05
HIGHEST = lax.Precision.HIGHEST
F32 = jnp.float32
BF16 = jnp.bfloat16
SENT = F32
ROWS = ((0,), (0,))
COLS = ((1,), (1,))
INNER_DIMS = ((1,), (0,))
VMEM_LIMIT = 48 * 1024 * 1024


def dot(left, right, dims=INNER_DIMS, precision=None):
    return lax.dot_general(left, right, (dims, ((), ())), precision=precision, preferred_element_type=F32)


def halves(value):
    high = value.astype(BF16)
    return high, (value - high.astype(F32)).astype(BF16)


def spread_operand(value):
    high, low = halves(value)
    return jnp.concatenate([high, low], axis=1)


def by_lane(first, second):
    low = iota(first.shape, 1) < STATE
    twice = jnp.where(low, first, second)
    high = twice.astype(BF16).astype(F32)
    return jnp.where(low, high, twice - high)


def twice(value, axis):
    return jnp.concatenate([value, value], axis=axis)


def fold(value):
    return value[:STATE] + value[STATE:]


def head_sums(value, selector):
    high, low = halves(value)
    return dot(high, selector) + dot(low, selector)


def sigmoid(value):
    return 1.0 / (1.0 + jnp.exp(-value))


def softplus(value):
    tail = jnp.exp(-jnp.abs(value))
    series = tail * (1.0 - tail * (0.5 - tail * (1.0 / 3.0 - 0.25 * tail)))
    return jnp.maximum(value, 0.0) + jnp.where(tail < 0.01, series, jnp.log(1.0 + tail))


def iota(shape, dim):
    return lax.broadcasted_iota(jnp.int32, shape, dim)


def span_scalars(info, m):
    first = info[2 * m]
    start = ((first + (BLOCK - 1)) >> 7) << 7
    return first, start, start + info[2 * m + 1], info[2 * MB], info[2 * MB + 1]


def keeps(info, m):
    _, start, _, base, span = span_scalars(info, m)

    def keep(position):
        begins = (position == 0) | (position == start) | (position >= span)
        return jnp.where(begins, 0.0, 1.0).astype(F32)

    forward = [keep(base), keep(base + BLOCK)]
    reverse = [keep(base + BLOCK), keep(base + 2 * BLOCK)]
    return forward, reverse


def row_masks(info, m, shape):
    first, start, end, base, _ = span_scalars(info, m)
    place = iota(shape, 0) + base
    inside = (place < first) | ((place >= start) & (place < end))
    offset = jnp.where(place >= start, place - start, place)
    return inside.astype(F32), [(offset >= k).astype(F32) for k in range(CONV)]


def conv_windows(ref, cols):
    main = ref[0, :TOK_DEV, cols]
    halo = ref[0, TOK_DEV:, cols]
    whole = jnp.concatenate([halo, main], axis=0)
    return [main] + [whole[HALO - k : HALO - k + TOK_DEV] for k in range(1, CONV)]


def conv_value(windows, masks, taps, cols):
    value = taps[CONV : CONV + 1, cols] + taps[0:1, cols] * windows[0]
    for k in range(1, CONV):
        value = value + taps[k : k + 1, cols] * (windows[k] * masks[k])
    return value


def front_kernel(info, vals, bc, dt, taps, steps, spread_f, spread_r, v_out, bc_out, fr_out, frp_out, tot_f, tot_r, kept_f, kept_r, dx_out):
    m = pl.program_id(0)
    valid, masks = row_masks(info, m, (TOK_DEV, LANES))
    for chunk in range(PAIRS + 1):
        cols = pl.ds(chunk * LANES, LANES)
        source, own = (vals, cols) if chunk < PAIRS else (bc, pl.ds(0, LANES))
        value = conv_value(conv_windows(source, own), masks, taps, cols)
        value = valid * (value * sigmoid(value))
        if chunk < PAIRS:
            v_out[0, :, cols] = value.astype(BF16)
        else:
            bc_out[0] = value
    lane = iota((BLOCK, LANES), 1)
    rows = iota((BLOCK, BLOCK), 0)
    columns = iota((BLOCK, BLOCK), 1)
    lower = (rows >= columns).astype(F32)
    upper = (rows <= columns).astype(F32)
    forward, reverse = keeps(info, m)
    ends = []
    tails = []
    inputs = []
    for b in range(2):
        span = pl.ds(b * BLOCK, BLOCK)
        step = softplus(dt[0, span, :] + steps[0:1, :])
        log = -step * steps[1:2, :]
        summed = jnp.where(lane < HEADS, dot(lower, log, precision=HIGHEST), dot(upper, log, precision=HIGHEST))
        shifted = summed - jnp.log(step)
        fr_out[0, span, :] = summed
        frp_out[0, span, :] = shifted
        end = jnp.where(lane[:1] < HEADS, summed[BLOCK - 1 :], summed[:1])
        ends.append(jnp.exp(end))
        tails.append(spread_operand(jnp.where(lane < 2 * HEADS, jnp.exp(end - shifted), 0.0)))
        acts = bc_out[0, span, :]
        inputs.append(twice(jnp.transpose(by_lane(acts, swapped(acts))).astype(BF16), 1))
    ends = spread_operand(jnp.concatenate(ends + [jnp.zeros((6, LANES), F32)], axis=0))
    width = 2 * LANES
    for chunk in range(INNER // width):
        cols = pl.ds(chunk * width, width)
        decay_f = dot(ends, spread_f[:, cols])
        decay_r = dot(ends, spread_r[:, cols])
        parts_f = []
        parts_r = []
        for b in range(2):
            v = v_out[0, pl.ds(b * BLOCK, BLOCK), cols].astype(F32)
            parts_f.append(fold(dot(inputs[b], stacked(dot(tails[b], spread_f[:, cols]) * v))))
            parts_r.append(fold(dot(inputs[b], stacked(dot(tails[b], spread_r[:, cols]) * v))))
        kept_f[0, :, cols] = parts_f[0]
        kept_r[0, :, cols] = parts_r[1]
        tot_f[0, :, cols] = (parts_f[1] + (forward[1] * decay_f[1:2]) * parts_f[0]).astype(SENT)
        tot_r[0, :, cols] = (parts_r[0] + (reverse[0] * decay_r[0:1]) * parts_r[1]).astype(SENT)
        dx_out[0, 0:2, cols] = decay_f[0:2]
        dx_out[0, 2:4, cols] = decay_r[0:2]
        dx_out[0, 4:5, cols] = (forward[0] * forward[1]) * (decay_f[0:1] * decay_f[1:2])
        dx_out[0, 5:6, cols] = (reverse[0] * reverse[1]) * (decay_r[0:1] * decay_r[1:2])
        dx_out[0, 6:8, cols] = jnp.zeros((2, width), F32)


def stacked(value):
    return jnp.concatenate(halves(value), axis=0)


def doubled(value):
    high, low = halves(value)
    return jnp.concatenate([high, high, low, low], axis=0)


def pair_stack(value):
    lane = iota(value.shape, 1)
    zero = jnp.zeros_like(value)
    return jnp.concatenate([jnp.where(lane < HEAD_DIM, value, zero), jnp.where(lane < HEAD_DIM, zero, value)], axis=0)


def swapped(value):
    return pltpu.roll(value, STATE, axis=1)


def intra_kernel(v, bc, fr, frp, skip, y_out):
    rows = iota((BLOCK, BLOCK), 0)
    columns = iota((BLOCK, BLOCK), 1)
    lower = rows > columns
    acts = bc[0]
    outs = jnp.where(columns < STATE, swapped(acts), 0.0)
    scores = jnp.where(rows == columns, 0.0, dot(outs, acts, COLS, HIGHEST))
    cum = fr[0]
    shifted = jnp.transpose(frp[0])
    for pair in range(PAIRS):
        mats = []
        for h in (2 * pair, 2 * pair + 1):
            r = HEADS + h
            gap = jnp.where(lower, cum[:, h : h + 1] - shifted[h : h + 1], cum[:, r : r + 1] - shifted[r : r + 1])
            mats.append((jnp.exp(gap) * scores).astype(BF16))
        cols = pl.ds(pair * LANES, LANES)
        value = v[0, :, cols]
        y = dot(jnp.concatenate(mats, axis=1), pair_stack(value))
        y_out[0, :, cols] = y + skip[0:1, cols] * value.astype(F32)


def entering(b, cols, forward, reverse, enter_f, enter_r, kept_f, kept_r, dx):
    first_f = forward[0] * enter_f[0, :, cols].astype(F32)
    last_r = reverse[1] * enter_r[0, :, cols].astype(F32)
    state_f = jnp.where(b == 0, first_f, forward[1] * (dx[0, 0:1, cols] * first_f + kept_f[0, :, cols]))
    state_r = jnp.where(b == 1, last_r, reverse[0] * (dx[0, 3:4, cols] * last_r + kept_r[0, :, cols]))
    return state_f, state_r


def middle_kernel(
    info, y, gate, d_normed, v, bc, fr, enter_f, enter_r, kept_f, kept_r, dx, gain, spread_f, spread_r, sum_f, sum_r,
    normed, d_mixed, d_gate, back_f, back_r, leave_f, leave_r, d_outs, read_out, d_gain, d_skip, mixed_s, part_f, part_r, exp_f, exp_r,
):
    m, b = pl.program_id(0), pl.program_id(1)
    forward, reverse = keeps(info, m)
    lane = iota((BLOCK, LANES), 1)
    outs = by_lane(swapped(bc[0]), bc[0])
    outs_t = twice(jnp.transpose(outs).astype(BF16), 1)
    outs = twice(outs.astype(BF16), 1)
    grown = spread_operand(jnp.where(lane < 2 * HEADS, jnp.exp(fr[0]), 0.0))
    width = 2 * LANES
    chunks = INNER // width
    squares = jnp.zeros((BLOCK, 1), F32)
    cross = jnp.zeros((BLOCK, 1), F32)
    for chunk in range(chunks):
        cols = pl.ds(chunk * width, width)
        state_f, state_r = entering(b, cols, forward, reverse, enter_f, enter_r, kept_f, kept_r, dx)
        ef = dot(grown, spread_f[:, cols])
        er = dot(grown, spread_r[:, cols])
        carried_f = ef * dot(outs, doubled(state_f))
        carried_r = er * dot(outs, doubled(state_r))
        mixed = y[0, :, cols] + carried_f + carried_r
        exp_f[:, cols] = ef
        exp_r[:, cols] = er
        part_f[:, cols] = carried_f
        part_r[:, cols] = carried_r
        mixed_s[:, cols] = mixed
        g = gate[0, :, cols]
        gated = mixed * (g * sigmoid(g))
        squares = squares + jnp.sum(gated * gated, axis=1, keepdims=True)
        cross = cross + jnp.sum(gated * gain[0:1, cols] * d_normed[0, :, cols], axis=1, keepdims=True)
    scale = lax.rsqrt(squares * (1.0 / INNER) + EPSILON)
    pull = scale * scale * scale * (cross * (1.0 / INNER))
    d_o = jnp.zeros((BLOCK, LANES), F32)
    reads = jnp.zeros((BLOCK, LANES), F32)

    @pl.when((m == 0) & (b == 0))
    def _():
        d_gain[...] = jnp.zeros_like(d_gain)
        d_skip[...] = jnp.zeros_like(d_skip)

    @pl.when(b == 0)
    def _():
        leave_f[...] = jnp.zeros_like(leave_f)
        leave_r[...] = jnp.zeros_like(leave_r)

    for chunk in range(chunks):
        cols = pl.ds(chunk * width, width)
        g = gate[0, :, cols]
        sig = sigmoid(g)
        silu = g * sig
        mixed = mixed_s[:, cols]
        gated = mixed * silu
        dy = d_normed[0, :, cols]
        scaled = gated * scale
        normed[0, :, cols] = (scaled * gain[0:1, cols]).astype(BF16)
        d_gain[0:1, cols] += jnp.sum(dy * scaled, axis=0, keepdims=True)
        d_gated = scale * gain[0:1, cols] * dy - gated * pull
        dm = d_gated * silu
        d_gate[0, :, cols] = (d_gated * mixed * sig * (1.0 + g * (1.0 - sig))).astype(BF16)
        d_mixed[0, :, cols] = dm.astype(BF16)
        d_skip[0:1, cols] += jnp.sum(dm * v[0, :, cols].astype(F32), axis=0, keepdims=True)
        state_f, state_r = entering(b, cols, forward, reverse, enter_f, enter_r, kept_f, kept_r, dx)
        grown_f = exp_f[:, cols] * dm
        grown_r = exp_r[:, cols] * dm
        local_f = fold(dot(outs_t, stacked(grown_f)))
        local_r = fold(dot(outs_t, stacked(grown_r)))
        back_f[0, 0, :, cols] = local_f
        back_r[0, 0, :, cols] = local_r
        weight_f = jnp.where(b == 0, forward[0], (forward[0] * forward[1]) * dx[0, 0:1, cols])
        weight_r = jnp.where(b == 0, (reverse[0] * reverse[1]) * dx[0, 3:4, cols], reverse[1])
        leave_f[0, :, cols] += weight_f * local_f
        leave_r[0, :, cols] += weight_r * local_r
        d_o = d_o + dot(spread_operand(grown_f), twice(stacked(state_f), 1), COLS)
        d_o = d_o + dot(spread_operand(grown_r), twice(stacked(state_r), 1), COLS)
        reads = reads + head_sums(dm * part_f[:, cols], sum_f[cols, :]) + head_sums(dm * part_r[:, cols], sum_r[cols, :])
    d_outs[0] = jnp.where(lane < STATE, 0.0, d_o + swapped(d_o))
    read_out[0] = reads


def intra_back_kernel(v, d_mixed, bc, fr, frp, skip, d_outs, read_out, d_v, d_bc, sums, d_log, row_s):
    rows = iota((BLOCK, BLOCK), 0)
    columns = iota((BLOCK, BLOCK), 1)
    ahead = rows < columns
    acts = bc[0]
    low = columns < STATE
    turned = swapped(acts)
    outs = jnp.where(low, turned, 0.0)
    scores = jnp.where(rows == columns, 0.0, dot(acts, outs, COLS, HIGHEST))
    cum = jnp.transpose(fr[0])
    shifted = frp[0]
    d_scores = jnp.zeros((BLOCK, BLOCK), F32)
    gathered = jnp.zeros((BLOCK, LANES), F32)

    row_s[...] = jnp.zeros_like(row_s)
    for pair in range(PAIRS):
        cols = pl.ds(pair * LANES, LANES)
        value = v[0, :, cols]
        dm = d_mixed[0, :, cols]
        products = dot(pair_stack(value), dm, COLS)
        mats = []
        for side in range(2):
            h = 2 * pair + side
            r = HEADS + h
            gap = jnp.where(ahead, cum[h : h + 1] - shifted[:, h : h + 1], cum[r : r + 1] - shifted[:, r : r + 1])
            weight = jnp.exp(gap)
            mats.append((weight * scores).astype(BF16))
            reach = products[side * BLOCK : (side + 1) * BLOCK] * weight
            d_scores = d_scores + reach
            both = reach * scores
            first = jnp.where(ahead, both, 0.0)
            second = both - first
            gathered = jnp.where(columns == h, jnp.sum(first, axis=1, keepdims=True), gathered)
            gathered = jnp.where(columns == r, jnp.sum(second, axis=1, keepdims=True), gathered)
            row_s[h : h + 1, :] = jnp.sum(first, axis=0, keepdims=True)
            row_s[r : r + 1, :] = jnp.sum(second, axis=0, keepdims=True)
        dmf = dm.astype(F32)
        d_v[0, :, cols] = dot(jnp.concatenate(mats, axis=1), pair_stack(dm)) + skip[0:1, cols] * dmf
    d_scores = jnp.where(rows == columns, 0.0, d_scores)
    ins = jnp.where(low, 0.0, turned)
    d_bc[0] = dot(d_scores, outs, precision=HIGHEST) + dot(jnp.transpose(d_scores), ins, precision=HIGHEST) + d_outs[0]
    sums[0] = gathered
    d_log[0] = jnp.transpose(row_s[...]) - gathered + read_out[0]


def final_kernel(
    info, vals, bc_in, dt, taps, steps, v, bc, fr, frp, enter_f, enter_r, kept_f, kept_r, dx, after_f, after_r, back_f, back_r,
    d_v, d_bc, sums, d_log, spread_f, spread_r, sum_f, sum_r,
    late, before, last, d_taps, d_small, d_acts,
):
    m = pl.program_id(0)
    forward, reverse = keeps(info, m)
    lane = iota((BLOCK, LANES), 1)
    row = iota((BLOCK, LANES), 0)
    rows = iota((BLOCK, BLOCK), 0)
    columns = iota((BLOCK, BLOCK), 1)
    lower = (rows >= columns).astype(F32)
    upper = (rows <= columns).astype(F32)
    width = 2 * LANES

    @pl.when(m == 0)
    def _():
        d_taps[...] = jnp.zeros_like(d_taps)
        d_small[...] = jnp.zeros_like(d_small)

    for b in range(2):
        span = pl.ds(b * BLOCK, BLOCK)
        summed = fr[0, span, :]
        end = jnp.where(lane[:1] < HEADS, summed[BLOCK - 1 :], summed[:1])
        tail = spread_operand(jnp.where(lane < 2 * HEADS, jnp.exp(end - frp[0, span, :]), 0.0))
        acts = bc[0, span, :]
        ins = twice(by_lane(acts, swapped(acts)).astype(BF16), 1)
        d_in = jnp.zeros((BLOCK, LANES), F32)
        used = jnp.zeros((BLOCK, LANES), F32)
        decays = jnp.zeros((8, LANES), F32)
        for chunk in range(INNER // width):
            cols = pl.ds(chunk * width, width)
            grad_f = after_f[0, :, cols].astype(F32)
            grad_r = after_r[0, :, cols].astype(F32)
            if b == 0:
                grad_f = forward[1] * (back_f[0, 1, :, cols] + dx[0, 1:2, cols] * grad_f)
            else:
                grad_r = reverse[0] * (back_r[0, 0, :, cols] + dx[0, 2:3, cols] * grad_r)
            state_f, state_r = entering(b, cols, forward, reverse, enter_f, enter_r, kept_f, kept_r, dx)
            tail_f = dot(tail, spread_f[:, cols])
            tail_r = dot(tail, spread_r[:, cols])
            value = v[0, span, cols].astype(F32)
            pulled_f = tail_f * dot(ins, doubled(grad_f))
            pulled_r = tail_r * dot(ins, doubled(grad_r))
            d_acts[span, cols] = d_v[0, span, cols] + pulled_f + pulled_r
            d_in = d_in + dot(spread_operand(tail_f * value), twice(stacked(grad_f), 1), COLS)
            d_in = d_in + dot(spread_operand(tail_r * value), twice(stacked(grad_r), 1), COLS)
            used = used + head_sums(pulled_f * value, sum_f[cols, :]) + head_sums(pulled_r * value, sum_r[cols, :])
            meet_f = jnp.sum(grad_f * state_f, axis=0, keepdims=True) * dx[0, b : b + 1, cols]
            meet_r = jnp.sum(grad_r * state_r, axis=0, keepdims=True) * dx[0, 2 + b : 3 + b, cols]
            zero = jnp.zeros((7, width), F32)
            decays = decays + head_sums(jnp.concatenate([meet_f, zero], axis=0), sum_f[cols, :])
            decays = decays + head_sums(jnp.concatenate([meet_r, zero], axis=0), sum_r[cols, :])
        d_acts[span, pl.ds(INNER, LANES)] = d_bc[0, span, :] + jnp.where(lane < STATE, d_in + swapped(d_in), 0.0)
        direct = sums[0, span, :] + used
        edge = decays[0:1] + jnp.sum(used, axis=0, keepdims=True)
        at_end = ((lane < HEADS) & (row == BLOCK - 1)) | ((lane >= HEADS) & (row == 0))
        grad = d_log[0, span, :] - used + jnp.where(at_end, edge, 0.0)
        grad = jnp.where(lane < HEADS, dot(upper, grad, precision=HIGHEST), dot(lower, grad, precision=HIGHEST))
        x = dt[0, span, :] + steps[0:1, :]
        step = softplus(x)
        sig = sigmoid(x)
        ratio = jnp.where(x < -17.0, 1.0, sig / step)
        d_x = direct * ratio - steps[1:2, :] * grad * sig
        d_x = jnp.where(lane < 2 * HEADS, d_x, 0.0)
        late[0, span, pl.ds(INNER + LANES, LANES)] = d_x.astype(BF16)
        d_small[0:1, :] += jnp.sum(d_x, axis=0, keepdims=True)
        d_small[1:2, :] -= steps[1:2, :] * jnp.sum(step * grad, axis=0, keepdims=True)
    valid, masks = row_masks(info, m, (TOK_DEV, LANES))
    edge = jnp.zeros((HALO, LANES), F32)
    for chunk in range(PAIRS + 1):
        cols = pl.ds(chunk * LANES, LANES)
        source, own = (vals, cols) if chunk < PAIRS else (bc_in, pl.ds(0, LANES))
        windows = conv_windows(source, own)
        value = conv_value(windows, masks, taps, cols)
        sig = sigmoid(value)
        grad = valid * d_acts[:, cols] * (sig * (1.0 + value * (1.0 - sig)))
        total = jnp.zeros((HALO + TOK_DEV, LANES), F32)
        for k in range(CONV):
            masked = grad if k == 0 else grad * masks[k]
            d_taps[k : k + 1, cols] += jnp.sum(masked * windows[k], axis=0, keepdims=True)
            padded = jnp.concatenate([edge, masked, edge], axis=0)
            total = total + taps[k : k + 1, cols] * padded[k : k + HALO + TOK_DEV]
        d_taps[CONV : CONV + 1, cols] += jnp.sum(grad, axis=0, keepdims=True)
        before[0, :, cols] = total[:HALO]
        last[0, :, cols] = total[TOK_DEV:]
        late[0, :, cols] = total[HALO:].astype(BF16)


def once(shape):
    return pl.BlockSpec(shape, lambda *grid: (0,) * len(shape))


def per_micro(shape, column=0):
    return pl.BlockSpec((1,) + shape, lambda m, *rest: (m,) + (0,) * (len(shape) - 1) + (column,))


def per_block(width, column=0):
    return pl.BlockSpec((1, BLOCK, width), lambda m, b: (m, b, column))


def struct(*shape, dtype=F32):
    return jax.ShapeDtypeStruct(shape, dtype)


SCALARS = pl.BlockSpec(memory_space=pltpu.SMEM)


def call(kernel, grid, in_specs, out_specs, out_shape, scratch=(), flops=0, moved=0):
    return pl.pallas_call(
        kernel,
        grid=grid,
        in_specs=in_specs,
        out_specs=out_specs,
        out_shape=out_shape,
        scratch_shapes=list(scratch),
        compiler_params=pltpu.CompilerParams(vmem_limit_bytes=VMEM_LIMIT),
        cost_estimate=pl.CostEstimate(flops=flops, bytes_accessed=moved, transcendentals=0),
    )


def shift(value, distance):
    count = lax.axis_size("dp")
    route = [(i, i + distance) for i in range(count) if 0 <= i + distance < count]
    return lax.ppermute(value, "dp", route)


def carry_kernel(
    levels, up_row, down_row, up_in, down_in, gains_in, up_out, down_out,
    up_other, down_other, gains_other, up_chain, down_chain, up_next, down_next,
    up_sems, down_sems, gain_sems, up_link, down_link,
):
    me = lax.axis_index("dp")
    side = lax.rem(me, 2)
    level = me // 2
    partner = me + 1 - 2 * side
    above, below = me + 2, me - 2
    has_above, has_below = level < levels - 1, level > 0

    barrier = pltpu.get_barrier_semaphore()
    pl.semaphore_signal(barrier, inc=1, device_id={"dp": partner})

    @pl.when(has_above)
    def _():
        pl.semaphore_signal(barrier, inc=1, device_id={"dp": above})

    @pl.when(has_below)
    def _():
        pl.semaphore_signal(barrier, inc=1, device_id={"dp": below})

    pl.semaphore_wait(barrier, 1 + has_above.astype(jnp.int32) + has_below.astype(jnp.int32))

    def remote(source, target, sems, k, device):
        return pltpu.make_async_remote_copy(
            src_ref=source, dst_ref=target, send_sem=sems.at[0, k], recv_sem=sems.at[1, k], device_id={"dp": device}
        )

    def swap_up(k):
        return remote(up_in.at[k], up_other.at[k], up_sems, k, partner)

    def swap_down(k):
        return remote(down_in.at[k], down_other.at[k], down_sems, k, partner)

    def climb(k):
        return remote(up_next.at[k], up_chain.at[k], up_link, k, above)

    def descend(k):
        return remote(down_next.at[k], down_chain.at[k], down_link, k, below)

    swap_gains = remote(gains_in, gains_other, gain_sems, 0, partner)
    swap_gains.start()

    @pl.loop(0, CHUNKS)
    def _(k):
        swap_up(k).start()
        swap_down(k).start()

    @pl.when(level == 0)
    def _():
        up_chain[...] = jnp.zeros_like(up_chain)

    @pl.when(level == levels - 1)
    def _():
        down_chain[...] = jnp.zeros_like(down_chain)

    swap_gains.wait()
    first = side == 0

    @pl.loop(0, CHUNKS + levels - 1)
    def _(s):
        up, down = s - level, s - (levels - 1 - level)

        @pl.when((up >= 0) & (up < CHUNKS))
        def _():
            swap_up(up).wait()

            @pl.when(has_below)
            def _():
                climb(up).wait_recv()

            m = up // PARTS
            own, other = gains_in[m, up_row : up_row + 1], gains_other[m, up_row : up_row + 1]
            near, far = jnp.where(first, own, other), jnp.where(first, other, own)
            mine, theirs = up_in[up], up_other[up]
            before = up_chain[up]
            middle = jnp.where(first, mine, theirs) + near * before
            up_out[up] = jnp.where(first, before, middle)

            @pl.when(has_above)
            def _():
                up_next[up] = jnp.where(first, theirs, mine) + far * middle
                climb(up).start()

        @pl.when((down >= 0) & (down < CHUNKS))
        def _():
            swap_down(down).wait()

            @pl.when(has_above)
            def _():
                descend(down).wait_recv()

            m = down // PARTS
            own, other = gains_in[m, down_row : down_row + 1], gains_other[m, down_row : down_row + 1]
            near, far = jnp.where(first, other, own), jnp.where(first, own, other)
            mine, theirs = down_in[down], down_other[down]
            before = down_chain[down]
            middle = jnp.where(first, theirs, mine) + near * before
            down_out[down] = jnp.where(first, middle, before)

            @pl.when(has_below)
            def _():
                down_next[down] = jnp.where(first, mine, theirs) + far * middle
                descend(down).start()

    @pl.when(has_above)
    def _():
        @pl.loop(0, CHUNKS)
        def _(k):
            climb(k).wait_send()

    @pl.when(has_below)
    def _():
        @pl.loop(0, CHUNKS)
        def _(k):
            descend(k).wait_send()


def carry(up, down, gains, up_row, down_row, identity):
    levels = lax.axis_size("dp") // 2
    shape = (CHUNKS, STATE // PARTS, INNER)
    buffer = pltpu.VMEM(shape, F32)
    outs = pl.pallas_call(
        partial(carry_kernel, levels, up_row, down_row),
        in_specs=[pl.BlockSpec(memory_space=pltpu.VMEM)] * 3,
        out_specs=[pl.BlockSpec(memory_space=pltpu.VMEM)] * 2,
        out_shape=[struct(*shape), struct(*shape)],
        scratch_shapes=[buffer, buffer, pltpu.VMEM((MB, 8, INNER), F32), buffer, buffer, buffer, buffer]
        + [pltpu.SemaphoreType.DMA((2, CHUNKS))] * 2
        + [pltpu.SemaphoreType.DMA((2, 1))]
        + [pltpu.SemaphoreType.DMA((2, CHUNKS))] * 2,
        compiler_params=pltpu.CompilerParams(vmem_limit_bytes=VMEM_LIMIT, collective_id=identity, has_side_effects=True),
    )(up.reshape(shape), down.reshape(shape), gains)
    return [out.reshape(MB, STATE, INNER) for out in outs]


def total_kernel(
    levels, columns, first_in, second_in, third_in, taps_in, scale_in, skip_in, small_in, norm_in, selector,
    first_out, inner_out, state_out, step_out, norm_out, taps_out, bias_out, steps_out, decay_out, skip_out, scale_out,
    mate_got, cross_put, cross_got, third_sum, fourth_sum,
    put_1y, got_1y, put_1z, got_1z, sum_1, all_1,
    put_2z, got_2z, put_2y, got_2y, sum_2, all_2,
    put_3y, got_3y, put_3z, got_3z, all_3,
    put_4z, got_4z, put_4y, got_4y, all_4, short_sum, short_got, short_sems,
    mate_sems, cross_sems, side_sems, level_sems,
):
    me, part = lax.axis_index("dp"), lax.axis_index("fsdp")
    side, level = lax.rem(me, 2), me // 2
    core, column = lax.rem(part, 2), part // 2
    partner = me + 1 - 2 * side
    mate = part + 1 - 2 * core

    def level_at(d):
        return lax.rem(level + d + levels, levels)

    def column_at(d):
        return lax.rem(column + d + columns, columns)

    def device(at):
        return {"dp": 2 * level_at(at) + side}

    barrier = pltpu.get_barrier_semaphore()
    pl.semaphore_signal(barrier, inc=1, device_id={"dp": partner})
    pl.semaphore_signal(barrier, inc=1, device_id={"fsdp": mate})
    for d in range(1, levels):
        pl.semaphore_signal(barrier, inc=1, device_id=device(d))
    for d in range(1, columns):
        pl.semaphore_signal(barrier, inc=1, device_id={"fsdp": 2 * column_at(d) + core})
    pl.semaphore_wait(barrier, levels + columns)

    def remote(source, target, sems, k, where):
        return pltpu.make_async_remote_copy(
            src_ref=source, dst_ref=target, send_sem=sems.at[0, k], recv_sem=sems.at[1, k], device_id=where
        )

    waiting = []

    def start(copy):
        copy.start()
        waiting.append(copy)

    def beside(source, target, k):
        return remote(source, target, side_sems, k, {"dp": partner})

    def scatter(put, got, k, d):
        return remote(put.at[level_at(d)], got.at[level], level_sems, k * levels + d, device(d))

    def scattered(put, got, k, d):
        return remote(put.at[level_at(d)], got.at[level_at(-d)], level_sems, k * levels + d, device(d))

    def gather(pick, k, d):
        return remote(pick(level), pick(level), level_sems, k * levels + d, device(d))

    def gathered(pick, k, d):
        return remote(pick(level), pick(level_at(-d)), level_sems, k * levels + d, device(d))

    for x in range(columns):
        start(remote(third_in.at[2 * x + 1 - core], mate_got.at[x], mate_sems, x, {"fsdp": mate}))

    lane = iota((8, LANES), 1)
    summed = jnp.where(lane < HEADS, head_sums(skip_in[...], selector[...]), 0.0)
    folded = small_in[...] + pltpu.roll(small_in[...], LANES - HEADS, axis=1)
    short_sum[0, 0:8, :] = taps_in[...]
    short_sum[0, 8:16, :] = jnp.zeros((8, CONV_COLS), F32)
    short_sum[0, 5:6, :INNER] = scale_in[0:1]
    short_sum[0, 6:7, :D] = norm_in[...]
    short_sum[0, 8:9, :LANES] = small_in[0:1]
    short_sum[0, 9:10, :LANES] = folded[1:2]
    short_sum[0, 10:11, :LANES] = summed[0:1]
    routes = [{"fsdp": mate}, {"dp": partner}]
    stride = 1
    while stride < columns:
        routes.append({"fsdp": part + 2 * stride - 4 * stride * lax.rem(column // stride, 2)})
        stride *= 2
    stride = 1
    while stride < levels:
        routes.append({"dp": me + 2 * stride - 4 * stride * lax.rem(level // stride, 2)})
        stride *= 2

    def short(k):
        return remote(short_sum.at[k], short_got.at[k], short_sems, k, routes[k])

    def short_step(k):
        if k > 0:
            short(k - 1).wait_recv()
            short_sum[k] = short_sum[k - 1] + short_got[k - 1]
        if k < len(routes):
            start(short(k))

    short_step(0)
    put_1y[...] = first_in[1 - side].astype(BF16)
    start(beside(put_1y, got_1y, 0))
    half = put_2z.shape[-1]
    for d in range(1, levels):
        target = level_at(d)
        for h in range(2):
            put_2z[target, h] = second_in[target, :, h * half : (h + 1) * half].astype(BF16)
        start(scatter(put_2z, got_2z, 0, d))

    short_step(1)
    rows, width = third_sum.shape[2], third_sum.shape[3]
    for x in range(columns):
        remote(third_in.at[2 * x + 1 - core], mate_got.at[x], mate_sems, x, {"fsdp": mate}).wait_recv()
    for d in range(1, columns):
        x = column_at(d)
        cross_put[x] = (third_in[2 * x + core] + mate_got[x]).astype(BF16)
        start(remote(cross_put.at[x], cross_got.at[column], cross_sems, d, {"fsdp": 2 * x + core}))

    short_step(2)
    beside(put_1y, got_1y, 0).wait_recv()
    sum_1[...] = first_in[side] + got_1y[...].astype(F32)
    for d in range(1, levels):
        target = level_at(d)
        put_1z[target] = sum_1[target].astype(BF16)
        start(scatter(put_1z, got_1z, 1, d))

    short_step(3)
    total = [second_in[level, :, h * half : (h + 1) * half] for h in range(2)]
    for d in range(1, levels):
        scattered(put_2z, got_2z, 0, d).wait_recv()
        for h in range(2):
            total[h] = total[h] + got_2z[level_at(-d), h].astype(F32)
    first = side == 0
    put_2y[...] = jnp.where(first, total[1], total[0]).astype(BF16)
    sum_2[...] = jnp.where(first, total[0], total[1])
    start(beside(put_2y, got_2y, 1))

    for d in range(1, columns):
        remote(cross_put.at[column_at(d)], cross_got.at[column_at(-d)], cross_sems, d, {"fsdp": part}).wait_recv()
    for x in range(2):
        for j in range(levels):
            at = pl.ds((x * levels + j) * rows, rows)
            value = third_in[part, at, :] + mate_got[column, at, :]
            for d in range(1, columns):
                value = value + cross_got[column_at(-d), at, :].astype(F32)
            third_sum[x, j] = value[:, :width]
            place = x * levels + j
            fourth_sum[place // 2, place % 2] = value[:, width:]

    short_step(4)
    put_3y[...] = third_sum[1 - side].astype(BF16)
    start(beside(put_3y, got_3y, 2))
    for d in range(1, levels):
        target = level_at(d)
        put_4z[target] = fourth_sum[target].astype(BF16)
        start(scatter(put_4z, got_4z, 2, d))

    total = sum_1[level]
    for d in range(1, levels):
        scattered(put_1z, got_1z, 1, d).wait_recv()
        total = total + got_1z[level_at(-d)].astype(F32)
    all_1[side, level] = total.astype(BF16)
    for d in range(1, levels):
        start(gather(lambda at: all_1.at[side, at], 3, d))

    for k in range(5, len(routes) + 1):
        short_step(k)
    result = short_sum.at[len(routes)]
    for f in range(2 * columns):

        @pl.when(part == f)
        def _():
            def own(row, rows, width, ref):
                size = width // (2 * columns)
                ref[...] = result[row : row + rows, f * size : (f + 1) * size]

            own(0, CONV, CONV_COLS, taps_out)
            own(4, 1, CONV_COLS, bias_out)
            own(5, 1, INNER, scale_out)
            own(6, 1, D, norm_out)
            own(8, 1, 2 * HEADS, steps_out)
            own(9, 1, HEADS, decay_out)
            own(10, 1, HEADS, skip_out)

    beside(put_2y, got_2y, 1).wait_recv()
    all_2[level, side] = (sum_2[...] + got_2y[...].astype(F32)).astype(BF16)
    start(beside(all_2.at[level, side], all_2.at[level, side], 3))

    beside(put_3y, got_3y, 2).wait_recv()
    third_sum[side] = third_sum[side] + got_3y[...].astype(F32)
    for d in range(1, levels):
        target = level_at(d)
        put_3z[target] = third_sum[side, target].astype(BF16)
        start(scatter(put_3z, got_3z, 4, d))

    total = fourth_sum[level]
    for d in range(1, levels):
        scattered(put_4z, got_4z, 2, d).wait_recv()
        total = total + got_4z[level_at(-d)].astype(F32)
    fourth_sum[level] = total
    put_4y[...] = fourth_sum[level, 1 - side].astype(BF16)
    start(beside(put_4y, got_4y, 4))

    for d in range(1, levels):
        gathered(lambda at: all_1.at[side, at], 3, d).wait_recv()
    start(beside(all_1.at[side], all_1.at[side], 5))
    beside(all_2.at[level, side], all_2.at[level, 1 - side], 3).wait_recv()
    for d in range(1, levels):
        start(gather(lambda at: all_2.at[at], 5, d))

    total = third_sum[side, level]
    for d in range(1, levels):
        scattered(put_3z, got_3z, 4, d).wait_recv()
        total = total + got_3z[level_at(-d)].astype(F32)
    all_3[side, level] = total.astype(BF16)
    for d in range(1, levels):
        start(gather(lambda at: all_3.at[side, at], 6, d))

    beside(put_4y, got_4y, 4).wait_recv()
    all_4[level, side] = (fourth_sum[level, side] + got_4y[...].astype(F32)).astype(BF16)
    start(beside(all_4.at[level, side], all_4.at[level, side], 6))

    beside(all_1.at[side], all_1.at[1 - side], 5).wait_recv()
    first_out[...] = all_1[...].astype(F32)
    for d in range(1, levels):
        gathered(lambda at: all_2.at[at], 5, d).wait_recv()
    for h in range(2):
        for j in range(levels):
            inner_out[j * 2 * rows : (j + 1) * 2 * rows, h * half : (h + 1) * half] = all_2[j, h].astype(F32)

    for d in range(1, levels):
        gathered(lambda at: all_3.at[side, at], 6, d).wait_recv()
    start(beside(all_3.at[side], all_3.at[side], 7))
    beside(all_4.at[level, side], all_4.at[level, 1 - side], 6).wait_recv()
    for d in range(1, levels):
        start(gather(lambda at: all_4.at[at], 7, d))
    beside(all_3.at[side], all_3.at[1 - side], 7).wait_recv()
    for d in range(1, levels):
        gathered(lambda at: all_4.at[at], 7, d).wait_recv()
    for x in range(2):
        for j in range(levels):
            place = x * levels + j
            at = pl.ds(place * rows, rows)
            inner_out[at, INNER : INNER + width] = all_3[x, j].astype(F32)
            value = all_4[place // 2, place % 2].astype(F32)
            inner_out[at, INNER + width :] = value[:, : INNER - width]
            state_out[at, :] = value[:, INNER - width : INNER - width + LANES]
            step_out[at, :] = value[:, INNER - width + LANES : INNER - width + LANES + 2 * HEADS]
    for copy in waiting:
        copy.wait_send()


def total_fits(levels, shards, dp_count):
    rows = D // shards
    return dp_count == 2 * levels and shards % 2 == 0 and rows % (16 * levels) == 0 and 24 % shards == 0


def totals(first, second, third, short, identity):
    dp_count, shards = lax.axis_size("dp"), lax.axis_size("fsdp")
    levels, columns = dp_count // 2, shards // 2
    rows = D // shards
    piece = rows // levels
    small = piece // 2
    width = LATE // 2
    steps = (dp_count * shards).bit_length() - 1

    def low(*shape):
        return pltpu.VMEM(shape, BF16)

    def full(*shape):
        return pltpu.VMEM(shape, F32)

    outs = pl.pallas_call(
        partial(total_kernel, levels, columns),
        in_specs=[pl.BlockSpec(memory_space=pltpu.VMEM)] * 9,
        out_specs=[pl.BlockSpec(memory_space=pltpu.VMEM)] * 11,
        out_shape=[struct(2, levels, piece, D), struct(rows, 2 * INNER), struct(rows, 2 * STATE), struct(rows, 2 * HEADS)]
        + [struct(1, D // shards), struct(CONV, CONV_COLS // shards), struct(1, CONV_COLS // shards)]
        + [struct(1, width // shards) for width in (2 * HEADS, HEADS, HEADS, INNER)],
        scratch_shapes=[
            full(columns, rows, LATE), low(columns, rows, LATE), low(columns, rows, LATE),
            full(2, levels, small, width), full(levels, 2, small, width),
            low(levels, piece, D), low(levels, piece, D), low(levels, piece, D), low(levels, piece, D),
            full(levels, piece, D), low(2, levels, piece, D),
            low(levels, 2, piece, D), low(levels, 2, piece, D), low(piece, D), low(piece, D),
            full(piece, D), low(levels, 2, piece, D),
            low(levels, small, width), low(levels, small, width), low(levels, small, width), low(levels, small, width),
            low(2, levels, small, width),
            low(levels, 2, small, width), low(levels, 2, small, width), low(small, width), low(small, width),
            low(levels, 2, small, width),
            full(steps + 1, 16, CONV_COLS), full(steps, 16, CONV_COLS), pltpu.SemaphoreType.DMA((2, steps)),
            pltpu.SemaphoreType.DMA((2, columns)), pltpu.SemaphoreType.DMA((2, columns)),
            pltpu.SemaphoreType.DMA((2, 8)), pltpu.SemaphoreType.DMA((2, 8 * levels)),
        ],
        compiler_params=pltpu.CompilerParams(vmem_limit_bytes=VMEM_LIMIT, collective_id=identity, has_side_effects=True),
    )(
        first.reshape(2, levels, piece, D), second.reshape(levels, piece, INNER), third.reshape(shards, rows, LATE), *short,
    )
    flat = [out.reshape(-1) for out in outs[6:]]
    return [outs[4].reshape(-1)] + list(outs[1:4]) + [outs[5]] + flat + [outs[0].reshape(2 * rows, D)]


def rms(values):
    return lax.rsqrt(jnp.mean(values * values, axis=-1, keepdims=True) + EPSILON)


def gather_small(parts):
    flat = jnp.concatenate([part.reshape(-1) for part in parts])
    size = flat.shape[0]
    padded = -(-size // LANES) * LANES
    everything = lax.all_gather(jnp.pad(flat, (0, padded - size)).reshape(1, padded), "fsdp", axis=0, tiled=True)
    result = []
    at = 0
    for part in parts:
        piece = everything[:, at : at + part.size].astype(F32)
        at += part.size
        if part.ndim == 2:
            piece = piece.reshape(-1, *part.shape).transpose(1, 0, 2).reshape(part.shape[0], -1)
        else:
            piece = piece.reshape(-1)
        result.append(piece)
    return result


def scatter_small(parts, shards):
    rows = []
    for part in parts:
        if part.ndim == 2:
            rows.append(part.reshape(part.shape[0], shards, -1).transpose(1, 0, 2).reshape(shards, -1))
        else:
            rows.append(part.reshape(shards, -1))
    flat = jnp.concatenate(rows, axis=1)
    size = flat.shape[1]
    padded = -(-size // LANES) * LANES
    return jnp.pad(flat, ((0, 0), (0, padded - size)))


def on_device(
    tokens, seq_lengths, norm_gain, w_inner, w_state, w_step, conv_weight, conv_bias, step_bias, decay_log, skip_gain, out_gain, w_out, cotangent,
):
    dp_count = lax.axis_size("dp")
    shards = lax.axis_size("fsdp")
    base = lax.axis_index("dp") * TOK_DEV
    lengths = seq_lengths[:, 0]
    info = jnp.concatenate([lengths.reshape(-1), jnp.stack([base, jnp.int32(dp_count * TOK_DEV)]).astype(jnp.int32)])
    mine = jnp.concatenate([w_inner, w_state, w_step, jnp.zeros((w_step.shape[0], WIDE - 2 * INNER - 2 * STATE - 2 * HEADS), BF16)], axis=1)
    w_all = lax.all_gather(mine, "fsdp", axis=0, tiled=True)
    gain_in, weight_conv, bias_conv, bias_steps, log_decay, gain_skip, gain_out = gather_small(
        (norm_gain, conv_weight, conv_bias, step_bias, decay_log, skip_gain, out_gain)
    )
    w_all, w_later = lax.optimization_barrier((w_all, w_out))
    w_back = lax.all_gather(w_later, "fsdp", axis=0, tiled=True)

    taps = jnp.concatenate([weight_conv, bias_conv[None], jnp.zeros((3, CONV_COLS), F32)], axis=0)
    rates = jnp.exp(log_decay)
    steps = jnp.zeros((8, LANES), F32).at[0, : 2 * HEADS].set(bias_steps).at[1, : 2 * HEADS].set(jnp.concatenate([rates, rates]))
    skip = jnp.broadcast_to(jnp.repeat(gain_skip, HEAD_DIM)[None], (8, INNER))
    out_scale = jnp.broadcast_to(gain_out[None], (8, INNER))
    head_of = jnp.arange(INNER, dtype=jnp.int32) // HEAD_DIM
    lanes = jnp.arange(LANES, dtype=jnp.int32)
    sum_f = (head_of[:, None] == lanes[None, :]).astype(BF16)
    sum_r = (head_of[:, None] + HEADS == lanes[None, :]).astype(BF16)
    both = jnp.concatenate([lanes, lanes])
    spread_f = (both[:, None] == head_of[None, :]).astype(BF16)
    spread_r = (both[:, None] == head_of[None, :] + HEADS).astype(BF16)

    x = tokens[:, 0]
    halo = shift(x[:, TOK_DEV - HALO :], 1)
    x_all = jnp.concatenate([x, halo], axis=1).astype(F32)
    hidden = (x_all * rms(x_all) * gain_in).astype(BF16)
    rows = TOK_DEV + HALO
    zx = jnp.dot(hidden.reshape(MB * rows, D), w_all, preferred_element_type=F32).reshape(MB, rows, WIDE)

    places = base + jnp.arange(TOK_DEV, dtype=jnp.int32)
    first = lengths[:, :1]
    start = (first + BLOCK - 1) // BLOCK * BLOCK
    valid = (places[None] < first) | (places[None] >= start) & (places[None] < start + lengths[:, 1:])
    valid = valid[..., None]
    cot = cotangent[:, 0]
    d_branch = jnp.where(valid, cot, jnp.zeros_like(cot)).reshape(MB * TOK_DEV, D)
    d_normed = dot(d_branch, w_back, COLS).reshape(MB, TOK_DEV, INNER)

    zx_vals = per_micro((rows, INNER), 1)
    zx_bc = per_micro((rows, LANES), 2 * INNER // LANES)
    zx_dt = per_micro((rows, LANES), 2 * INNER // LANES + 1)
    taps_spec, steps_spec = once((8, CONV_COLS)), once((8, LANES))
    spread_spec, sum_spec = once((2 * LANES, INNER)), once((INNER, LANES))
    state_spec, dx_spec = per_micro((STATE, INNER)), per_micro((8, INNER))
    wide_spec, lane_spec = per_micro((TOK_DEV, INNER)), per_micro((TOK_DEV, LANES))
    v, bc, fr, frp, tot_f, tot_r, kept_f, kept_r, dx = call(
        front_kernel,
        (MB,),
        [SCALARS, zx_vals, zx_bc, zx_dt, taps_spec, steps_spec, spread_spec, spread_spec],
        [wide_spec, lane_spec, lane_spec, lane_spec, state_spec, state_spec, state_spec, state_spec, dx_spec],
        [
            struct(MB, TOK_DEV, INNER, dtype=BF16),
            struct(MB, TOK_DEV, LANES),
            struct(MB, TOK_DEV, LANES),
            struct(MB, TOK_DEV, LANES),
            struct(MB, STATE, INNER, dtype=SENT),
            struct(MB, STATE, INNER, dtype=SENT),
            struct(MB, STATE, INNER),
            struct(MB, STATE, INNER),
            struct(MB, 8, INNER),
        ],
        flops=1_000_000_000,
        moved=20_000_000,
    )(info, zx, zx, zx, taps, steps, spread_f, spread_r)

    enter_f, enter_r = carry(tot_f, tot_r, dx, 4, 5, 0)

    y = call(
        intra_kernel,
        (MB, 2),
        [per_block(INNER), per_block(LANES), per_block(LANES), per_block(LANES), once((8, INNER))],
        per_block(INNER),
        struct(MB, TOK_DEV, INNER),
        flops=20_000_000_000,
        moved=8_000_000,
    )(v, bc, fr, frp, skip)

    back_spec = pl.BlockSpec((1, 1, STATE, INNER), lambda m, b: (m, b, 0, 0))
    normed, d_mixed, d_gate, back_f, back_r, leave_f, leave_r, d_outs, read_out, d_out_gain, d_skip = call(
        middle_kernel,
        (MB, 2),
        [SCALARS, per_block(INNER), per_block(INNER), per_block(INNER), per_block(INNER), per_block(LANES), per_block(LANES)]
        + [state_spec] * 4
        + [dx_spec, once((8, INNER)), spread_spec, spread_spec, sum_spec, sum_spec],
        [per_block(INNER)] * 3 + [back_spec, back_spec, state_spec, state_spec, per_block(LANES), per_block(LANES), once((8, INNER)), once((8, INNER))],
        [
            struct(MB, TOK_DEV, INNER, dtype=BF16),
            struct(MB, TOK_DEV, INNER, dtype=BF16),
            struct(MB, TOK_DEV, INNER, dtype=BF16),
            struct(MB, 2, STATE, INNER),
            struct(MB, 2, STATE, INNER),
            struct(MB, STATE, INNER),
            struct(MB, STATE, INNER),
            struct(MB, TOK_DEV, LANES),
            struct(MB, TOK_DEV, LANES),
            struct(8, INNER),
            struct(8, INNER),
        ],
        scratch=[pltpu.VMEM((BLOCK, INNER), F32)] * 5,
        flops=2_000_000_000,
        moved=30_000_000,
    )(info, y, zx, d_normed, v, bc, fr, enter_f, enter_r, kept_f, kept_r, dx, out_scale, spread_f, spread_r, sum_f, sum_r)

    after_r, after_f = carry(leave_r, leave_f, dx, 5, 4, 1)

    d_v, d_bc, sums, d_log = call(
        intra_back_kernel,
        (MB, 2),
        [per_block(INNER), per_block(INNER), per_block(LANES), per_block(LANES), per_block(LANES), once((8, INNER)), per_block(LANES), per_block(LANES)],
        [per_block(INNER), per_block(LANES), per_block(LANES), per_block(LANES)],
        [struct(MB, TOK_DEV, INNER)] + [struct(MB, TOK_DEV, LANES)] * 3,
        scratch=[pltpu.VMEM((BLOCK, LANES), F32)],
        flops=30_000_000_000,
        moved=10_000_000,
    )(v, d_mixed, bc, fr, frp, skip, d_outs, read_out)

    late, before, last, d_taps, d_small = call(
        final_kernel,
        (MB,),
        [SCALARS, zx_vals, zx_bc, zx_dt, taps_spec, steps_spec, wide_spec, lane_spec, lane_spec, lane_spec]
        + [state_spec] * 4
        + [dx_spec, state_spec, state_spec, per_micro((2, STATE, INNER)), per_micro((2, STATE, INNER))]
        + [wide_spec, lane_spec, lane_spec, lane_spec, spread_spec, spread_spec, sum_spec, sum_spec],
        [per_micro((TOK_DEV, LATE)), per_micro((HALO, CONV_COLS)), per_micro((HALO, CONV_COLS)), once((8, CONV_COLS)), once((8, LANES))],
        [
            struct(MB, TOK_DEV, LATE, dtype=BF16),
            struct(MB, HALO, CONV_COLS),
            struct(MB, HALO, CONV_COLS),
            struct(8, CONV_COLS),
            struct(8, LANES),
        ],
        scratch=[pltpu.VMEM((TOK_DEV, CONV_COLS), F32)],
        flops=2_000_000_000,
        moved=40_000_000,
    )(
        info, zx, zx, zx, taps, steps, v, bc, fr, frp, enter_f, enter_r, kept_f, kept_r, dx, after_f, after_r, back_f, back_r,
        d_v, d_bc, sums, d_log, spread_f, spread_r, sum_f, sum_r,
    )
    ending = (last + shift(before, -1)).astype(BF16)
    late = lax.dynamic_update_slice(late, ending, (0, TOK_DEV - HALO, 0)).reshape(MB * TOK_DEV, LATE)

    hidden_low = hidden[:, :TOK_DEV].reshape(MB * TOK_DEV, D)
    d_gate = d_gate.reshape(MB * TOK_DEV, INNER)
    normed = normed.reshape(MB * TOK_DEV, INNER)
    branch = dot(normed, w_back).reshape(MB, TOK_DEV, D)
    x_rows = x.astype(F32)
    layer_out = jnp.where(valid, x_rows + branch, 0.0).astype(BF16)

    def owned(grad):
        return lax.psum_scatter(grad, "fsdp", scatter_dimension=0, tiled=True)

    first_grad = owned(dot(normed, d_branch, ROWS))
    gate_grad = owned(dot(hidden_low, d_gate, ROWS))
    late_grad = dot(hidden_low, late, ROWS)

    d_hidden = dot(d_gate, w_all[:, :INNER], COLS) + dot(late, w_all[:, INNER:], COLS)
    d_hidden = d_hidden.reshape(MB, TOK_DEV, D)
    scale = rms(x_rows)
    d_norm_gain = jnp.sum(d_hidden * x_rows * scale, axis=(0, 1))
    pulled = d_hidden * gain_in
    d_x = scale * pulled - x_rows * (scale * scale * scale) * jnp.mean(x_rows * pulled, axis=-1, keepdims=True)
    tokens_grad = d_x + jnp.where(valid, cot.astype(F32), 0.0)

    d_norm_gain = d_norm_gain[None]
    if total_fits(dp_count // 2, shards, dp_count):
        grads = totals(first_grad, gate_grad, late_grad, (d_taps, d_out_gain, d_skip, d_small, d_norm_gain, sum_f), 2)
    else:
        d_skip_gain = jnp.sum(d_skip[0].reshape(HEADS, HEAD_DIM), axis=1)
        d_decay = d_small[1, :HEADS] + d_small[1, HEADS : 2 * HEADS]
        small = (d_norm_gain[0], d_taps[:CONV], d_taps[CONV], d_small[0, : 2 * HEADS], d_decay, d_skip_gain, d_out_gain[0])
        w_out_grad, gate_grad, late_grad = lax.psum((first_grad, gate_grad, owned(late_grad)), "dp")
        summed = lax.psum(scatter_small(small, shards), ("dp", "fsdp"))
        own = lax.dynamic_slice_in_dim(summed, lax.axis_index("fsdp"), 1, axis=0)[0]
        pieces = []
        at = 0
        for part in (norm_gain, conv_weight, conv_bias, step_bias, decay_log, skip_gain, out_gain):
            pieces.append(own[at : at + part.size].reshape(part.shape))
            at += part.size
        w_inner_grad = jnp.concatenate([gate_grad, late_grad[:, :INNER]], axis=1)
        w_state_grad = late_grad[:, INNER : INNER + 2 * STATE]
        w_step_grad = late_grad[:, INNER + LANES : INNER + LANES + 2 * HEADS]
        grads = pieces[:1] + [w_inner_grad, w_state_grad, w_step_grad] + pieces[1:] + [w_out_grad]
    return (layer_out[:, None], tokens_grad[:, None], *grads)


def solution(mesh):
    rows, vector, matrix = P(None, "fsdp", "dp", None), P("fsdp"), P("fsdp", None)
    weights = (vector, matrix, matrix, matrix, P(None, "fsdp"), vector, vector, vector, vector, vector, matrix)
    return jax.shard_map(
        on_device,
        mesh=mesh,
        in_specs=(rows, P(None, "fsdp", None)) + weights + (rows,),
        out_specs=(rows, rows) + weights,
        check_vma=False,
    )
```

time: 1850 us -> 474 us (0.26)
  the two profiles are of different devices: /device:TPU:0 before, /device:TPU:10 now
where the time goes in v1:
time: 474 us; the launch traced here: 466 us
  Pallas kernels  318 us (67%)
  matrix products  41.9 us (9%)
  local copies, waits for them, and re-layouts  37.1 us (8%)
  waiting for transfers between devices  28.2 us (6%)
  between operations  14.7 us (3%)
  other arithmetic  11.3 us (2%)
  starting transfers between devices  9.48 us (2%)
  blocking collectives  5.22 us (1%)
    pallas_call x2, Pallas kernels, carry(): pl.pallas_call(partial(carry_kernel, levels, up_row, down_row), in_specs=...  139 us
    pallas_call x1, Pallas kernels, totals(): pl.pallas_call(partial(total_kernel, levels, columns), in_specs=[pl.Block...  81.6 us
    dot_general x7, matrix products, dot(): lax.dot_general(left, right, (dims, ((), ())), precision=precision, prefe...  32.1 us
    pallas_call x1, Pallas kernels, on_device(): call(final_kernel, (MB,), [SCALARS, zx_vals, zx_bc, zx_dt, taps_spec, ste...  30.1 us
    all_gather x1, waiting for transfers between devices, on_device(): w_all = lax.all_gather(mine, 'fsdp', axis=0, tiled=True)  28.2 us
    unnamed x94, local copies, waits for them, and re-layouts  26.7 us
    pallas_call x1, Pallas kernels, on_device(): call(intra_back_kernel, (MB, 2), [per_block(INNER), per_block(INNER), per...  24.5 us
    pallas_call x1, Pallas kernels, on_device(): call(middle_kernel, (MB, 2), [SCALARS, per_block(INNER), per_block(INNER)...  22.1 us
  transfers between devices with their start and end apart: 6, of which 1 were waited for; matrix products, arithmetic and copies ran while one was open for 10% of the time, Pallas kernels for 46%

profile of v1, /device:TPU:10, one launch (start us, length us, event | category | flops | bytes accessed | tf_op | source)
XLA Modules:
  0.0 466.4 jit_solution(6094621939618372233)
XLA Ops:
  8.2 3.2 concatenate.28
  12.2 3.4 collective-permute-start
  15.9 5.2 %all-gather.1 = bf16[4,1,2688]{2,1,0:T(2,128)(2,1)S(1)} all-gather(bf16[1,1,2688]{2,1,0:T(2,128)(2,1)S(1)} %reshape.437), channel_id=2, replica_groups=mesh['dp'=8,'fsdp'=4] {'fsdp'}, dimensions={0}, use_global_device_ids=true | all-gather | bytes 26880 | tf_op jit(solution)/shard_map/all_gather | solution.py:926
  23.3 28.2 %all-gather.5.cloned.1.call-done = bf16[768,3328]{1,0:T(8,128)(2,1)} async-done(((bf16[192,3328]{1,0:T(8,128)(2,1)}), bf16[768,3328]{1,0:T(8,128)(2,1)}) %all-gather.5.cloned.1.call-update) | async-done | bytes 5111824 | tf_op jit(solution)/shard_map/all_gather | solution.py:962
  52.3 1.6 fusion.4
  54.0 1.6 fusion.6
  55.6 9.8 %fusion.vals.bc.dt.gate.bc_in = f32[3,264,3328]{2,1,0:T(8,128)} fusion(bf16[3,264,768]{2,1,0:T(8,128)(2,1)S(1)} %fusion.6, bf16[768,3328]{1,0:T(8,128)(2,1)} %all-gather.5.cloned.1.call-done), kind=kOutput, calls=%fused_computation | convolution fusion | flops 4048551936 | bytes 16871424 | tf_op jit(solution)/shard_map/dot_general | solution.py:987
  65.4 12.4 %shard_map.237 = (bf16[3,256,1536]{2,1,0:T(8,128)(2,1)}, f32[3,256,128]{2,1,0:T(8,128)S(1)}, f32[3,256,128]{2,1,0:T(8,128)S(1)}, f32[3,256,128]{2,1,0:T(8,128)S(...) custom-call(s32[8]{0:T(128)S(1)} %pad_add_fusion.1.info, ...), custom_call_target="tpu_custom_call" | custom-call | flops 1000000000 | bytes 20000000 | tf_op jit(solution)/shard_map/pallas_call | solution.py:1005
  77.8 72.0 %shard_map.239 = (f32[6,32,1536]{2,1,0:T(8,128)S(1)}, f32[6,32,1536]{2,1,0:T(8,128)S(1)}) custom-call(f32[6,32,1536]{2,1,0:T(8,128)S(1)} %bitcast.95, f32[6,32,1536]{2,1,0:T(8,128)S(1)} %bitcast.96, f32[3,8,1536]{2,1,0:T(8,128)S(1)} %get-tuple-element.91.gains_in.dx), custom_call_target="tpu_custom_call" | custom-call | tf_op jit(solution)/shard_map/pallas_call | solution.py:608
  151.8 8.4 %shard_map.238.y = f32[3,256,1536]{2,1,0:T(8,128)} custom-call(bf16[3,256,1536]{2,1,0:T(8,128)(2,1)S(1)} %copy-done, f32[3,256,128]{2,1,0:T(8,128)S(1)} %get-tuple-element.85.bc, f32[3,256,128]{2,1,0:T(8,128)S(1)} %get-tuple-element.86.fr, f32[3,256,128]{2,1,0:T(8,128)S(1)} %get-tuple-element.87.frp, f32[8,1536]{1,0:T(8,128)S(1)} %broadcast_in_dim.83.skip), custom_call_target="tpu_custom_call" | custom-call | flops 20000000000 | bytes 8000000 | tf_op jit(solution)/shard_map/pallas_call | solution.py:1027
  160.2 6.3 %fusion.15.d_normed = f32[3,256,1536]{2,1,0:T(8,128)} fusion(bf16[1536,768]{1,0:T(8,128)(2,1)} %all-gather.7.cloned.1.call-done, bf16[3,1,256,768]{3,2,1,0:T(8,128)(2,1)} %param.31, pred[3,256]{1,0:T(4,128)(4,1)S(1)} %and_or_fusion), kind=kOutput, calls=%fused_computation.23 | convolution fusion | flops 1812529152 | bytes 8258304 | tf_op jit(solution)/shard_map/dot_general | solution.py:39
  166.5 22.1 %shard_map.240 = (bf16[3,256,1536]{2,1,0:T(8,128)(2,1)}, bf16[3,256,1536]{2,1,0:T(8,128)(2,1)}, bf16[3,256,1536]{2,1,0:T(8,128)(2,1)}, f32[3,2,64,1536]{3,2,1,0:...) custom-call(s32[8]{0:T(128)S(1)} %pad_add_fusion.1.info, ...), custom_call_target="tpu_custom_call" | custom-call | flops 2000000000 | bytes 30000000 | tf_op jit(solution)/shard_map/pallas_call | solution.py:1038
  191.2 5.8 %convolution_bitcast_fusion = f32[768,1536]{1,0:T(8,128)} fusion(bf16[3,256,1536]{2,1,0:T(8,128)(2,1)} %get-tuple-element.97, bf16[3,264,768]{2,1,0:T(8,128)(2,1)S(1)} %copy-done.23), kind=kOutput, calls=%fused_computation.2 | convolution fusion | flops 1811939328 | bytes 8257536 | tf_op jit(solution)/shard_map/dot_general | solution.py:39
  197.1 6.3 %convolution_bitcast_fusion.1 = f32[1536,768]{1,0:T(8,128)} fusion(bf16[3,256,1536]{2,1,0:T(8,128)(2,1)} %get-tuple-element.96, bf16[3,1,256,768]{3,2,1,0:T(8,128)(2,1)} %param.31, pred[3,256]{1,0:T(4,128)(4,1)S(1)} %and_or_fusion), kind=kOutput, calls=%fused_computation.3 | convolution fusion | flops 1812529152 | bytes 8258304 | tf_op jit(solution)/shard_map/dot_general | solution.py:39
  203.4 2.5 slice.98
  205.8 2.6 copy.60
  208.5 1.5 copy-done.7
  210.0 1.3 copy-done.8
  211.2 67.4 %shard_map.241 = (f32[6,32,1536]{2,1,0:T(8,128)S(1)}, f32[6,32,1536]{2,1,0:T(8,128)S(1)}) custom-call(f32[6,32,1536]{2,1,0:T(8,128)S(1)} %bitcast.94, f32[6,32,1536]{2,1,0:T(8,128)S(1)} %bitcast.93, f32[3,8,1536]{2,1,0:T(8,128)S(1)} %get-tuple-element.91.gains_in.dx), custom_call_target="tpu_custom_call" | custom-call | tf_op jit(solution)/shard_map/pallas_call | solution.py:608
  283.7 24.5 %shard_map.242 = (f32[3,256,1536]{2,1,0:T(8,128)}, f32[3,256,128]{2,1,0:T(8,128)S(1)}, f32[3,256,128]{2,1,0:T(8,128)S(1)}, f32[3,256,128]{2,1,0:T(8,128)S(1)}) custom-call(bf16[3,256,1536]{2,1,0:T(8,128)(2,1)S(1)} %copy-done.1, bf16[3,256,1536]{2,1,0:T(8,128)(2,1)} %get-tuple-element.104.d_mixed, f32[3,256,128]{2,1,0:T(8,128)S(1)} %get-tuple-element.85.bc, ...), custom_call_target="tpu_custom_call" | custom-call | flops 30000001024 | bytes 10000000 | tf_op jit(solution)/shard_map/pallas_call | solution.py:1065
  308.2 30.1 %shard_map.243 = (bf16[3,256,1792]{2,1,0:T(8,128)(2,1)}, f32[3,8,1664]{2,1,0:T(8,128)S(1)}, f32[3,8,1664]{2,1,0:T(8,128)S(1)}, f32[8,1664]{1,0:T(8,128)S(1)}, f32[8,128]{1,0:T(8,128)S(1)}) custom-call(s32[8]{0:T(128)S(1)} %pad_add_fusion.1.info, f32[3,264,3328]{2,1,0:T(8,128)} %fusion.vals.bc.dt.gate.bc_in, f32[3,264,3328]{2,1,0:T(8,128)} %fusion.vals.bc.dt.gate.bc_in, ...), custom_call_target="tpu_custom_call" | custom-call | flops 2000000000 | bytes 40000000 | tf_op jit(solution)/shard_map/pallas_call | solution.py:1076
  338.3 5.9 %collective-permute-start.1 = (f32[3,8,1664]{2,1,0:T(8,128)S(1)}, f32[3,8,1664]{2,1,0:T(8,128)S(1)}, u32[]{:S(2)}, u32[]{:S(2)}) collective-permute-start(f32[3,8,1664]{2,1,0:T(8,128)S(1)} %get-tuple-element.113), channel_id=1, source_target_pairs={{4,0},{8,4},{12,8},{16,12},{20,16},{24,20},{28,24},{5,1},{9,5},{13... | collective-permute-start | bytes 479240 | tf_op jit(solution)/shard_map/ppermute | solution.py:481
  344.3 4.7 %fusion.24 = bf16[3,1,256,768]{3,2,1,0:T(8,128)(2,1)} fusion(bf16[3,256,1536]{2,1,0:T(8,128)(2,1)} %get-tuple-element.96, bf16[1536,768]{1,0:T(8,128)(2,1)S(1)} %copy-done.36, pred[3,256]{1,0:T(4,128)(4,1)S(1)} %and_or_fusion, bf16[3,1,256,768]{3,2,1,0:T(8,128)(2,1)S(1)} %copy-done.18), kind=kOutput, calls=%fused_computation.31 | convolution fusion | flops 1814298624 | bytes 7078656 | tf_op jit(solution)/shard_map/dot_general | solution.py:39
  349.0 2.0 fusion.17
  351.0 2.3 fusion.19
  355.5 2.2 fusion.12
  357.9 3.1 select_add_fusion
  361.0 4.7 %fusion.40.third_in = f32[4,192,1792]{2,1,0:T(8,128)} fusion(bf16[4,192,768]{2,1,0:T(8,128)(2,1)S(1)} %bitcast.111, bf16[768,1792,1]{1,0,2:T(8,128)(2,1)S(1)} %bitcast.125), kind=kOutput, calls=%fused_computation.79 | convolution fusion | flops 2113929216 | bytes 9437184 | tf_op jit(solution)/shard_map/dot_general | solution.py:39
  365.8 1.3 copy-done.9
  367.1 1.3 copy-done.10
  368.3 81.6 %shard_map.244 = (f32[2,4,48,768]{3,2,1,0:T(8,128)S(1)}, f32[192,3072]{1,0:T(8,128)}, f32[192,128]{1,0:T(8,128)S(1)}, f32[192,48]{1,0:T(8,128)S(1)}, f32[1,192]{...) custom-call(f32[2,4,48,768]{3,2,1,0:T(8,128)S(1)} %bitcast.99, ...), custom_call_target="tpu_custom_call" | custom-call | tf_op jit(solution)/shard_map/pallas_call | solution.py:888
  451.8 3.3 copy.82
  (153 shorter events, 23.3 us)
Async XLA Ops:
  7.2 8.5 %copy-start.26 = (bf16[4,416]{1,0:T(4,128)(2,1)S(1)}, bf16[4,416]{1,0:T(4,128)(2,1)}, u32[]{:S(2)}) copy-start(bf16[4,416]{1,0:T(4,128)(2,1)} %param.24) | copy-start | bytes 9988
  7.2 8.6 %copy-start.29 = (bf16[192]{0:T(256)(128)(2,1)S(1)}, bf16[192]{0:T(256)(128)(2,1)}, u32[]{:S(2)}) copy-start(bf16[192]{0:T(256)(128)(2,1)} %param.20) | copy-start | bytes 1156
  7.2 8.6 %copy-start.27 = (bf16[416]{0:T(512)(128)(2,1)S(1)}, bf16[416]{0:T(512)(128)(2,1)}, u32[]{:S(2)}) copy-start(bf16[416]{0:T(512)(128)(2,1)} %param.25) | copy-start | bytes 2500
  7.2 8.6 %copy-start.30 = (bf16[12]{0:T(256)(128)(2,1)S(1)}, bf16[12]{0:T(256)(128)(2,1)}, u32[]{:S(2)}) copy-start(bf16[12]{0:T(256)(128)(2,1)} %param.26) | copy-start | bytes 76
  7.2 8.6 %copy-start.31 = (bf16[6]{0:T(256)(128)(2,1)S(1)}, bf16[6]{0:T(256)(128)(2,1)}, u32[]{:S(2)}) copy-start(bf16[6]{0:T(256)(128)(2,1)} %param.27) | copy-start | bytes 40
  7.2 8.6 %copy-start.32 = (bf16[6]{0:T(256)(128)(2,1)S(1)}, bf16[6]{0:T(256)(128)(2,1)}, u32[]{:S(2)}) copy-start(bf16[6]{0:T(256)(128)(2,1)} %param.28) | copy-start | bytes 40
  7.2 8.6 %copy-start.28 = (bf16[384]{0:T(512)(128)(2,1)S(1)}, bf16[384]{0:T(512)(128)(2,1)}, u32[]{:S(2)}) copy-start(bf16[384]{0:T(512)(128)(2,1)} %param.29) | copy-start | bytes 2308
  7.3 14.8 %copy-start.25 = (s32[3,1,2]{0,2,1:T(2,128)S(1)}, s32[3,1,2]{0,2,1:T(2,128)}, u32[]{:S(2)}) copy-start(s32[3,1,2]{0,2,1:T(2,128)} %param.19) | copy-start | bytes 76
  7.3 44.2 %all-gather.5.cloned.1.call-start = ((), (), s32[]{:S(2)}) async-start(), calls=%async_computation.2 | async-start | bytes 6389760 | tf_op jit(solution)/shard_map/all_gather | solution.py:962
  11.4 148.8 %all-gather.7.cloned.1.call-start = ((), (), s32[]{:S(2)}) async-start(), calls=%async_computation.3 | async-start | bytes 2949120 | tf_op jit(solution)/shard_map/all_gather | solution.py:967
  12.2 40.1 %collective-permute-start = (bf16[3,8,768]{2,1,0:T(8,128)(2,1)S(1)}, bf16[3,8,768]{2,1,0:T(8,128)(2,1)S(1)}, u32[]{:S(2)}, u32[]{:S(2)}) collective-permute-start(bf16[3,8,768]{2,1,0:T(8,128)(2,1)S(1)} %slice.90), channel_id=1, source_target_pairs={{0,4},{4,8},{8,12},{12,16},{16,20},{20,24},{24,28},{1,5},{5,9},{9,... | collective-permute-start | bytes 110600 | tf_op jit(solution)/shard_map/ppermute | solution.py:481
  51.5 314.3 %reduce-scatter.5.cloned.1.call-start = ((), (), s32[]{:S(2)}) async-start(), calls=%async_computation.5 | async-start | bytes 5898240 | tf_op jit(solution)/shard_map/reduce_scatter | solution.py:1109
  55.6 9.8 %copy-start.22 = (bf16[3,264,768]{2,1,0:T(8,128)(2,1)}, bf16[3,264,768]{2,1,0:T(8,128)(2,1)S(1)}, u32[]{:S(2)}) copy-start(bf16[3,264,768]{2,1,0:T(8,128)(2,1)S(1)} %fusion.6) | copy-start | bytes 3649540
  77.8 74.0 %copy-start.11 = (f32[3,256,128]{2,1,0:T(8,128)}, f32[3,256,128]{2,1,0:T(8,128)S(1)}, u32[]{:S(2)}) copy-start(f32[3,256,128]{2,1,0:T(8,128)S(1)} %get-tuple-element.87.frp) | copy-start | bytes 1179652
  77.8 74.0 %copy-start = (bf16[3,256,1536]{2,1,0:T(8,128)(2,1)S(1)}, bf16[3,256,1536]{2,1,0:T(8,128)(2,1)}, u32[]{:S(2)}) copy-start(bf16[3,256,1536]{2,1,0:T(8,128)(2,1)} %get-tuple-element.84.v) | copy-start | bytes 7077892
  166.5 24.7 %copy-start.23 = (bf16[3,264,768]{2,1,0:T(8,128)(2,1)S(1)}, bf16[3,264,768]{2,1,0:T(8,128)(2,1)}, u32[]{:S(2)}) copy-start(bf16[3,264,768]{2,1,0:T(8,128)(2,1)} %copy-done.22) | copy-start | bytes 3649540
  197.0 168.8 %reduce-scatter.3.cloned.1.call-start = ((), (), s32[]{:S(2)}) async-start(), calls=%async_computation.4 | async-start | bytes 5898240 | tf_op jit(solution)/shard_map/reduce_scatter | solution.py:1109
  208.5 72.3 %copy-start.1 = (bf16[3,256,1536]{2,1,0:T(8,128)(2,1)S(1)}, bf16[3,256,1536]{2,1,0:T(8,128)(2,1)}, u32[]{:S(2)}) copy-start(bf16[3,256,1536]{2,1,0:T(8,128)(2,1)} %get-tuple-element.84.v) | copy-start | bytes 7077892
  208.5 1.5 copy-start.7
  283.7 24.5 %copy-start.13 = (f32[3,256,128]{2,1,0:T(8,128)S(1)}, f32[3,256,128]{2,1,0:T(8,128)}, u32[]{:S(2)}) copy-start(f32[3,256,128]{2,1,0:T(8,128)} %copy-done.11) | copy-start | bytes 1179652
  308.2 36.1 %copy-start.18 = (bf16[3,1,256,768]{3,2,1,0:T(8,128)(2,1)S(1)}, bf16[3,1,256,768]{3,2,1,0:T(8,128)(2,1)}, u32[]{:S(2)}) copy-start(bf16[3,1,256,768]{3,2,1,0:T(8,128)(2,1)} %param.18) | copy-start | bytes 3538948
  308.2 36.1 %copy-start.36 = (bf16[1536,768]{1,0:T(8,128)(2,1)S(1)}, bf16[1536,768]{1,0:T(8,128)(2,1)}, u32[]{:S(2)}) copy-start(bf16[1536,768]{1,0:T(8,128)(2,1)} %all-gather.7.cloned.1.call-done) | copy-start | bytes 7077892
  338.3 10.6 %slice-start = ((s8[5111808]{0:T(1024)(128)(4,1)}), s8[4194304]{0:T(1024)(128)(4,1)S(1)}, s32[]{:S(2)}) async-start(s8[5111808]{0:T(1024)(128)(4,1)} %bitcast.122), calls=%async_computation.6 | async-start | bytes 8388608
  338.3 10.6 %slice-start.1 = ((s8[5111808]{0:T(1024)(128)(4,1)}), s8[917504]{0:T(1024)(128)(4,1)S(1)}, s32[]{:S(2)}) async-start(s8[5111808]{0:T(1024)(128)(4,1)} %bitcast.122), calls=%async_computation.7 | async-start | bytes 1835008
  338.3 10.6 %copy-start.37 = (bf16[3,256,1536]{2,1,0:T(8,128)(2,1)S(1)}, bf16[3,256,1536]{2,1,0:T(8,128)(2,1)}, u32[]{:S(2)}) copy-start(bf16[3,256,1536]{2,1,0:T(8,128)(2,1)} %get-tuple-element.97) | copy-start | bytes 7077892
  338.3 12.7 %collective-permute-start.1 = (f32[3,8,1664]{2,1,0:T(8,128)S(1)}, f32[3,8,1664]{2,1,0:T(8,128)S(1)}, u32[]{:S(2)}, u32[]{:S(2)}) collective-permute-start(f32[3,8,1664]{2,1,0:T(8,128)S(1)} %get-tuple-element.113), channel_id=1, source_target_pairs={{4,0},{8,4},{12,8},{16,12},{20,16},{24,20},{28,24},{5,1},{9,5},{13... | collective-permute-start | bytes 479240 | tf_op jit(solution)/shard_map/ppermute | solution.py:481
  349.0 2.0 copy-start.33
  351.0 2.3 copy-start.34
  353.4 2.1 copy-start.19
  355.5 2.4 copy-start.21
  357.9 3.1 copy-start.24
  357.9 3.1 copy-start.35
  (14 other events, 14.9 us)
Sparse Core Ops, SparseCore 0:
  11.5 39.9 all-gather.4
  53.0 24.0 all-gather.6
  197.1 47.1 reduce-scatter.4
  246.8 47.8 reduce-scatter.2
